TPU v7x, 512 devices: a whole 4x8x8 slice. The times are simulated.
512 devices in a mesh: section: 2 (over core), dp: 256 (over z, y, x).
Axes of the slice: x: 4, y: 8, z: 8, core: 2. Of those that a mesh axis runs over, the one named last changes fastest.
Arguments:
- images: bfloat16 [4, 512, 8, 8, 512], P(None, 'dp'), may hold values from -6 to 6
- cotangent: bfloat16 [4, 512, 8, 8, 512], P(None, 'dp'), may hold values from -0.016479492 to 0.016479492
- counts: int32 [2], P('section'), may hold values from 1 to 4, as said below
- gains: float32 [8, 512], P('section'), may hold values from 0.1 to 1.9
- depthwise: float32 [8, 9, 512], P('section'), may hold values from -2 to 2
- pointwise: bfloat16 [8, 512, 512], P('section'), may hold values from -0.25 to 0.25
Outputs:
- grad_pointwise: float32 [8, 512, 512], P('section')
- grad_depthwise: float32 [8, 9, 512], P('section')
- grad_gains: float32 [8, 512], P('section')
Inputs may be any that keep to these rules, and one draw needn't show every extreme that they name: counts[s] is how many cells segment s applies, from its first slot on; at least one segment applies 4 cells.
All inputs are finite; a program needn't handle non-finite values.
Results may differ from a plain program's by a relative error of at most 0.0085.
Values may be sent and summed in bfloat16 or wider, within the bound.
No kernel may reach another device: no remote copies, remote signals or barrier semaphores. Data moves between devices by JAX's collectives and lax.ppermute only.
A program may use at most 64 MiB of HBM per device.

v0:
```python
from functools import partial
import math

import jax
import jax.numpy as jnp
from jax import lax
from jax.sharding import PartitionSpec as P

EPSILON = 1e-06


def passed_along(block, axis, distance):
    devices = range(lax.axis_size(axis))
    route = [(i - distance, i) for i in devices if i - distance in devices]
    return lax.ppermute(block, axis, route)


def depth_apply(normed, depth_w):
    kernel = math.isqrt(depth_w.shape[0])
    offset = kernel // 2
    height, map_width = (normed.shape[1], normed.shape[2])
    padded = jnp.pad(normed, ((0, 0), (offset, offset), (offset, offset), (0, 0)))
    summed = jnp.zeros_like(normed)
    for row_tap in range(kernel):
        for col_tap in range(kernel):
            summed = (
                summed
                + depth_w[row_tap * kernel + col_tap]
                * padded[:, row_tap : row_tap + height, col_tap : col_tap + map_width]
            )
    return summed


def cell_parts(cell_in, gain_row, depth_w):
    widened = cell_in.astype(jnp.float32)
    inverse = lax.rsqrt(jnp.mean(widened * widened, axis=-1, keepdims=True) + EPSILON)
    normed = widened * inverse * gain_row
    linear = depth_apply(normed, depth_w)
    activated = (linear * jax.nn.sigmoid(linear)).astype(jnp.bfloat16)
    return (widened, inverse, normed, linear, activated)


def cell_forward(cell_in, gain_row, depth_w, point_w):
    widened, inverse, normed, linear, activated = cell_parts(cell_in, gain_row, depth_w)
    channels = point_w.shape[0]
    mixed_sum = jnp.dot(
        activated.reshape(-1, channels), point_w, preferred_element_type=jnp.float32
    )
    return (widened + mixed_sum.reshape(widened.shape)).astype(jnp.bfloat16)


def cell_backward(cell_in, grad_out, gain_row, depth_w, point_w):
    widened, inverse, normed, linear, activated = cell_parts(cell_in, gain_row, depth_w)
    channels = point_w.shape[0]
    flat_act = activated.reshape(-1, channels)
    flat_grad = grad_out.reshape(-1, channels)
    grad_point = lax.dot_general(
        flat_act, flat_grad, (((0,), (0,)), ((), ())), preferred_element_type=jnp.float32
    )
    grad_act = lax.dot_general(
        flat_grad, point_w, (((1,), (1,)), ((), ())), preferred_element_type=jnp.float32
    ).reshape(widened.shape)
    sigma = jax.nn.sigmoid(linear)
    grad_linear = grad_act * (sigma * (1.0 + linear * (1.0 - sigma)))
    kernel = math.isqrt(depth_w.shape[0])
    offset = kernel // 2
    height, map_width = (normed.shape[1], normed.shape[2])
    padded = jnp.pad(normed, ((0, 0), (offset, offset), (offset, offset), (0, 0)))
    padded_grad = jnp.pad(grad_linear, ((0, 0), (offset, offset), (offset, offset), (0, 0)))
    tap_list = []
    grad_normed = jnp.zeros_like(grad_linear)
    for row_tap in range(kernel):
        for col_tap in range(kernel):
            tap_list.append(
                jnp.sum(
                    padded[:, row_tap : row_tap + height, col_tap : col_tap + map_width]
                    * grad_linear,
                    axis=(0, 1, 2),
                )
            )
            row_start = 2 * offset - row_tap
            col_start = 2 * offset - col_tap
            grad_normed = (
                grad_normed
                + depth_w[row_tap * kernel + col_tap]
                * padded_grad[:, row_start : row_start + height, col_start : col_start + map_width]
            )
    grad_depth = jnp.stack(tap_list)
    grad_gain = jnp.sum(grad_normed * widened * inverse, axis=(0, 1, 2))
    scaled = grad_normed * gain_row
    grad_in = (
        grad_out.astype(jnp.float32)
        + inverse * scaled
        - widened * inverse**3 * jnp.mean(scaled * widened, axis=-1, keepdims=True)
    )
    return (grad_in.astype(jnp.bfloat16), grad_point, grad_depth, grad_gain)


def keep_value(passed):
    return passed


def backward_slot(operands, gain_row, depth_w, point_w):
    return cell_backward(operands[0], operands[1], gain_row, depth_w, point_w)


def pass_slot(operands, gain_row, depth_w, point_w):
    channels = point_w.shape[0]
    return (
        operands[1],
        jnp.zeros((channels, channels), jnp.float32),
        jnp.zeros(depth_w.shape, jnp.float32),
        jnp.zeros(gain_row.shape, jnp.float32),
    )


def local(images, cotangent, counts, gains, depthwise, pointwise):
    segment_count = lax.axis_size("section")
    segment_index = lax.axis_index("section")
    cell_count = counts[0]
    slot_total = gains.shape[0]
    group_total = images.shape[0]
    step_count = group_total + segment_count - 1
    item_shape = images.shape[1:]

    def cell_chain(segment_in, limit):
        cell_inputs = []
        current = segment_in
        for slot_number in range(limit):
            cell_inputs.append(current)
            forward_fn = partial(
                cell_forward,
                gain_row=gains[slot_number],
                depth_w=depthwise[slot_number],
                point_w=pointwise[slot_number],
            )
            current = lax.cond(slot_number < cell_count, forward_fn, keep_value, current)
        return (current, cell_inputs)

    def run_forward(segment_in):
        segment_out, cell_inputs = cell_chain(segment_in, slot_total)
        return (segment_out, jnp.stack(cell_inputs))

    def skip_forward(segment_in):
        return (segment_in, jnp.zeros((slot_total,) + segment_in.shape, jnp.bfloat16))

    saved_init = jnp.zeros((group_total,) + item_shape, jnp.bfloat16)

    def forward_step(loop_state, step_index):
        incoming, saved = loop_state
        group_index = step_index - segment_index
        active = (group_index >= 0) & (group_index < group_total)
        clipped = jnp.clip(group_index, 0, group_total - 1)
        fresh_rows = lax.dynamic_index_in_dim(images, clipped, 0, keepdims=False)
        segment_in = jnp.where(segment_index == 0, fresh_rows, incoming)
        segment_out, cell_inputs = lax.cond(active, run_forward, skip_forward, segment_in)
        current = lax.dynamic_index_in_dim(saved, clipped, 0, keepdims=False)
        saved = lax.dynamic_update_index_in_dim(
            saved, jnp.where(active, segment_in, current), clipped, 0
        )
        outgoing = passed_along(segment_out, "section", 1)
        return ((outgoing, saved), None)

    steps_list = jnp.arange(step_count, dtype=jnp.int32)
    empty_rows = jnp.zeros(item_shape, jnp.bfloat16)
    (unused_rows, saved), unused_out = lax.scan(forward_step, (empty_rows, saved_init), steps_list)

    def run_backward(operands):
        record, grad_run = operands
        last_input, cell_inputs = cell_chain(record, slot_total - 1)
        cell_inputs = cell_inputs + [last_input]
        point_list = [None] * slot_total
        depth_list = [None] * slot_total
        gain_list = [None] * slot_total
        for slot_number in reversed(range(slot_total)):
            grad_run, point_list[slot_number], depth_list[slot_number], gain_list[slot_number] = (
                lax.cond(
                    slot_number < cell_count,
                    partial(
                        backward_slot,
                        gain_row=gains[slot_number],
                        depth_w=depthwise[slot_number],
                        point_w=pointwise[slot_number],
                    ),
                    partial(
                        pass_slot,
                        gain_row=gains[slot_number],
                        depth_w=depthwise[slot_number],
                        point_w=pointwise[slot_number],
                    ),
                    (cell_inputs[slot_number], grad_run),
                )
            )
        return (grad_run, jnp.stack(point_list), jnp.stack(depth_list), jnp.stack(gain_list))

    def skip_backward(operands):
        return (
            operands[1],
            jnp.zeros(pointwise.shape, jnp.float32),
            jnp.zeros(depthwise.shape, jnp.float32),
            jnp.zeros(gains.shape, jnp.float32),
        )

    def backward_step(loop_state, step_index):
        incoming, point_run, depth_run, gain_run = loop_state
        group_index = step_index - (segment_count - 1 - segment_index)
        active = (group_index >= 0) & (group_index < group_total)
        clipped = jnp.clip(group_index, 0, group_total - 1)
        fresh_rows = lax.dynamic_index_in_dim(cotangent, clipped, 0, keepdims=False)
        grad_in = jnp.where(segment_index == segment_count - 1, fresh_rows, incoming)
        record = lax.dynamic_index_in_dim(saved, clipped, 0, keepdims=False)
        grad_out, point_term, depth_term, gain_term = lax.cond(
            active, run_backward, skip_backward, (record, grad_in)
        )
        outgoing = passed_along(grad_out, "section", -1)
        return (
            (outgoing, point_run + point_term, depth_run + depth_term, gain_run + gain_term),
            None,
        )

    start_state = (
        empty_rows,
        jnp.zeros(pointwise.shape, jnp.float32),
        jnp.zeros(depthwise.shape, jnp.float32),
        jnp.zeros(gains.shape, jnp.float32),
    )
    (unused_grad, point_acc, depth_acc, gain_acc), unused_out = lax.scan(
        backward_step, start_state, steps_list
    )
    point_acc, depth_acc, gain_acc = lax.psum((point_acc, depth_acc, gain_acc), "dp")
    return (point_acc, depth_acc, gain_acc)


def solution(mesh):
    placed = (
        P(None, "dp", None, None, None),
        P(None, "dp", None, None, None),
        P("section"),
        P("section", None),
        P("section", None, None),
        P("section", None, None),
    )
    return jax.shard_map(
        local,
        mesh=mesh,
        in_specs=placed,
        out_specs=(P("section", None, None), P("section", None, None), P("section", None)),
        check_vma=False,
    )
```

profile of v0, /device:TPU:0, one launch (start us, length us, event | category | flops | bytes accessed | tf_op | source)
XLA Modules:
  0.0 1095.3 jit_solution(11112540762050898712)
XLA Ops:
  9.7 105.3 %while.32 = (s32[]{:T(128)}, bf16[2,8,8,512]{3,2,1,0:T(8,128)(2,1)S(1)}, bf16[4,2,8,8,512]{4,3,2,1,0:T(8,128)(2,1)}, s32[5]{0:T(128)S(1)}, s32[]{:T(128)}, /*ind...) while((s32[]{:T(128)}, ...), condition=%wide.region_15.16_spmd, body=%wide.region_0.15_spmd.sunk | while | flops 276693504 | bytes 7988232 | solution.py:166
  13.6 6.0 conditional.16
  31.8 12.4 %collective-permute-start = (bf16[2,8,8,512]{3,2,1,0:T(8,128)(2,1)S(1)}, bf16[2,8,8,512]{3,2,1,0:T(8,128)(2,1)S(1)}, u32[]{:S(2)}, u32[]{:S(2)}) collective-permute-start(bf16[2,8,8,512]{3,2,1,0:T(8,128)(2,1)S(1)} %get-tuple-element.1182), channel_id=1, source_target_pairs={{0,256},{1,257},{2,258},{3,259},{4,260},{5,261},{6,262},{7,263},{8... | collective-permute-start | bytes 393224 | tf_op jit(solution)/shard_map/while/body/eval_jaxpr/ppermute | solution.py:15
  55.1 12.4 %collective-permute-start = (bf16[2,8,8,512]{3,2,1,0:T(8,128)(2,1)S(1)}, bf16[2,8,8,512]{3,2,1,0:T(8,128)(2,1)S(1)}, u32[]{:S(2)}, u32[]{:S(2)}) collective-permute-start(bf16[2,8,8,512]{3,2,1,0:T(8,128)(2,1)S(1)} %get-tuple-element.1182), channel_id=1, source_target_pairs={{0,256},{1,257},{2,258},{3,259},{4,260},{5,261},{6,262},{7,263},{8... | collective-permute-start | bytes 393224 | tf_op jit(solution)/shard_map/while/body/eval_jaxpr/ppermute | solution.py:15
  78.3 12.4 %collective-permute-start = (bf16[2,8,8,512]{3,2,1,0:T(8,128)(2,1)S(1)}, bf16[2,8,8,512]{3,2,1,0:T(8,128)(2,1)S(1)}, u32[]{:S(2)}, u32[]{:S(2)}) collective-permute-start(bf16[2,8,8,512]{3,2,1,0:T(8,128)(2,1)S(1)} %get-tuple-element.1182), channel_id=1, source_target_pairs={{0,256},{1,257},{2,258},{3,259},{4,260},{5,261},{6,262},{7,263},{8... | collective-permute-start | bytes 393224 | tf_op jit(solution)/shard_map/while/body/eval_jaxpr/ppermute | solution.py:15
  95.6 18.4 %collective-permute-start = (bf16[2,8,8,512]{3,2,1,0:T(8,128)(2,1)S(1)}, bf16[2,8,8,512]{3,2,1,0:T(8,128)(2,1)S(1)}, u32[]{:S(2)}, u32[]{:S(2)}) collective-permute-start(bf16[2,8,8,512]{3,2,1,0:T(8,128)(2,1)S(1)} %get-tuple-element.1182), channel_id=1, source_target_pairs={{0,256},{1,257},{2,258},{3,259},{4,260},{5,261},{6,262},{7,263},{8... | collective-permute-start | bytes 393224 | tf_op jit(solution)/shard_map/while/body/eval_jaxpr/ppermute | solution.py:15
  115.5 264.6 %while.33 = (s32[]{:T(128)}, bf16[2,8,8,512]{3,2,1,0:T(8,128)(2,1)S(1)}, f32[4,512,512]{2,1,0:T(8,128)}, f32[4,9,512]{2,1,0:T(8,128)}, f32[4,512]{1,0:T(4,128)},...) while((s32[]{:T(128)}, ...), condition=%wide.region_84.85_spmd.clone, body=%wide.region_16.84_spmd.clone.sunk | while | flops 773015424 | bytes 57160892 | solution.py:227
  129.6 38.3 %collective-permute-done.1 = bf16[2,8,8,512]{3,2,1,0:T(8,128)(2,1)S(1)} collective-permute-done((bf16[2,8,8,512]{3,2,1,0:T(8,128)(2,1)}, bf16[2,8,8,512]{3,2,1,0:T(8,128)(2,1)S(1)}, u32[]{:S(2)}, u32[]{:S(2)}) %collective-permute-start.1) | collective-permute-done | bytes 131104 | tf_op jit(solution)/shard_map/while/body/eval_jaxpr/ppermute | solution.py:15
  171.3 24.3 %conditional.17 = (bf16[2,8,8,512]{3,2,1,0:T(8,128)(2,1)}, f32[4,512,512]{2,1,0:T(8,128)}, f32[4,9,512]{2,1,0:T(8,128)S(1)}, f32[4,512]{1,0:T(4,128)}) conditional(s32[]{:T(128)} %convert_element_type.353, bf16[2,8,8,512]{3,2,1,0:T(8,128)(2,1)} %bitcast_select_fusion.5, (s32[]{:T(128)}, bf16[4,2,8,8,512]{4,3,2,1,0:T(8,128)(2,1)}, s32[]{:T(128)}, ...), branch_computations={%region_17.17_spmd, %region_18.83_spmd} | conditional | flops 770811776 | bytes 42758896 | solution.py:212
  182.8 7.9 conditional.11
  196.9 6.6 select_add_fusion.6
  204.3 21.2 %collective-permute-done.1 = bf16[2,8,8,512]{3,2,1,0:T(8,128)(2,1)S(1)} collective-permute-done((bf16[2,8,8,512]{3,2,1,0:T(8,128)(2,1)}, bf16[2,8,8,512]{3,2,1,0:T(8,128)(2,1)S(1)}, u32[]{:S(2)}, u32[]{:S(2)}) %collective-permute-start.1) | collective-permute-done | bytes 131104 | tf_op jit(solution)/shard_map/while/body/eval_jaxpr/ppermute | solution.py:15
  228.8 24.3 %conditional.17 = (bf16[2,8,8,512]{3,2,1,0:T(8,128)(2,1)}, f32[4,512,512]{2,1,0:T(8,128)}, f32[4,9,512]{2,1,0:T(8,128)S(1)}, f32[4,512]{1,0:T(4,128)}) conditional(s32[]{:T(128)} %convert_element_type.353, bf16[2,8,8,512]{3,2,1,0:T(8,128)(2,1)} %bitcast_select_fusion.5, (s32[]{:T(128)}, bf16[4,2,8,8,512]{4,3,2,1,0:T(8,128)(2,1)}, s32[]{:T(128)}, ...), branch_computations={%region_17.17_spmd, %region_18.83_spmd} | conditional | flops 770811776 | bytes 42758896 | solution.py:212
  240.3 7.9 conditional.11
  254.4 6.6 select_add_fusion.6
  261.8 22.4 %collective-permute-done.1 = bf16[2,8,8,512]{3,2,1,0:T(8,128)(2,1)S(1)} collective-permute-done((bf16[2,8,8,512]{3,2,1,0:T(8,128)(2,1)}, bf16[2,8,8,512]{3,2,1,0:T(8,128)(2,1)S(1)}, u32[]{:S(2)}, u32[]{:S(2)}) %collective-permute-start.1) | collective-permute-done | bytes 131104 | tf_op jit(solution)/shard_map/while/body/eval_jaxpr/ppermute | solution.py:15
  287.6 24.3 %conditional.17 = (bf16[2,8,8,512]{3,2,1,0:T(8,128)(2,1)}, f32[4,512,512]{2,1,0:T(8,128)}, f32[4,9,512]{2,1,0:T(8,128)S(1)}, f32[4,512]{1,0:T(4,128)}) conditional(s32[]{:T(128)} %convert_element_type.353, bf16[2,8,8,512]{3,2,1,0:T(8,128)(2,1)} %bitcast_select_fusion.5, (s32[]{:T(128)}, bf16[4,2,8,8,512]{4,3,2,1,0:T(8,128)(2,1)}, s32[]{:T(128)}, ...), branch_computations={%region_17.17_spmd, %region_18.83_spmd} | conditional | flops 770811776 | bytes 42758896 | solution.py:212
  299.2 7.9 conditional.11
  313.2 6.6 select_add_fusion.6
  320.6 22.4 %collective-permute-done.1 = bf16[2,8,8,512]{3,2,1,0:T(8,128)(2,1)S(1)} collective-permute-done((bf16[2,8,8,512]{3,2,1,0:T(8,128)(2,1)}, bf16[2,8,8,512]{3,2,1,0:T(8,128)(2,1)S(1)}, u32[]{:S(2)}, u32[]{:S(2)}) %collective-permute-start.1) | collective-permute-done | bytes 131104 | tf_op jit(solution)/shard_map/while/body/eval_jaxpr/ppermute | solution.py:15
  346.5 24.3 %conditional.17 = (bf16[2,8,8,512]{3,2,1,0:T(8,128)(2,1)}, f32[4,512,512]{2,1,0:T(8,128)}, f32[4,9,512]{2,1,0:T(8,128)S(1)}, f32[4,512]{1,0:T(4,128)}) conditional(s32[]{:T(128)} %convert_element_type.353, bf16[2,8,8,512]{3,2,1,0:T(8,128)(2,1)} %bitcast_select_fusion.5, (s32[]{:T(128)}, bf16[4,2,8,8,512]{4,3,2,1,0:T(8,128)(2,1)}, s32[]{:T(128)}, ...), branch_computations={%region_17.17_spmd, %region_18.83_spmd} | conditional | flops 770811776 | bytes 42758896 | solution.py:212
  358.0 7.9 conditional.11
  372.1 6.6 select_add_fusion.6
  381.7 701.5 %psum.23 = f32[4,512]{1,0:T(4,128)} all-reduce(f32[4,512]{1,0:T(4,128)S(1)} %copy-done.9), channel_id=1, replica_groups=mesh['section'=2,'dp'=256] {'dp'}, use_global_device_ids=true, to_apply=%region_87.88 | all-reduce | flops 2048 | bytes 16384 | tf_op jit(solution)/shard_map/psum | solution.py:230
  (363 shorter events, 209.8 us)
Async XLA Ops:
  7.2 1076.0 %all-reduce.18.cloned.1.call-start = ((), (), s32[]{:S(2)}) async-start(), calls=%async_computation | async-start | bytes 8536064 | tf_op jit(solution)/shard_map/psum | solution.py:230
  19.6 2.3 collective-permute-start
  31.8 13.4 %collective-permute-start = (bf16[2,8,8,512]{3,2,1,0:T(8,128)(2,1)S(1)}, bf16[2,8,8,512]{3,2,1,0:T(8,128)(2,1)S(1)}, u32[]{:S(2)}, u32[]{:S(2)}) collective-permute-start(bf16[2,8,8,512]{3,2,1,0:T(8,128)(2,1)S(1)} %get-tuple-element.1182), channel_id=1, source_target_pairs={{0,256},{1,257},{2,258},{3,259},{4,260},{5,261},{6,262},{7,263},{8... | collective-permute-start | bytes 393224 | tf_op jit(solution)/shard_map/while/body/eval_jaxpr/ppermute | solution.py:15
  55.1 13.4 %collective-permute-start = (bf16[2,8,8,512]{3,2,1,0:T(8,128)(2,1)S(1)}, bf16[2,8,8,512]{3,2,1,0:T(8,128)(2,1)S(1)}, u32[]{:S(2)}, u32[]{:S(2)}) collective-permute-start(bf16[2,8,8,512]{3,2,1,0:T(8,128)(2,1)S(1)} %get-tuple-element.1182), channel_id=1, source_target_pairs={{0,256},{1,257},{2,258},{3,259},{4,260},{5,261},{6,262},{7,263},{8... | collective-permute-start | bytes 393224 | tf_op jit(solution)/shard_map/while/body/eval_jaxpr/ppermute | solution.py:15
  78.3 13.4 %collective-permute-start = (bf16[2,8,8,512]{3,2,1,0:T(8,128)(2,1)S(1)}, bf16[2,8,8,512]{3,2,1,0:T(8,128)(2,1)S(1)}, u32[]{:S(2)}, u32[]{:S(2)}) collective-permute-start(bf16[2,8,8,512]{3,2,1,0:T(8,128)(2,1)S(1)} %get-tuple-element.1182), channel_id=1, source_target_pairs={{0,256},{1,257},{2,258},{3,259},{4,260},{5,261},{6,262},{7,263},{8... | collective-permute-start | bytes 393224 | tf_op jit(solution)/shard_map/while/body/eval_jaxpr/ppermute | solution.py:15
  95.6 19.4 %collective-permute-start = (bf16[2,8,8,512]{3,2,1,0:T(8,128)(2,1)S(1)}, bf16[2,8,8,512]{3,2,1,0:T(8,128)(2,1)S(1)}, u32[]{:S(2)}, u32[]{:S(2)}) collective-permute-start(bf16[2,8,8,512]{3,2,1,0:T(8,128)(2,1)S(1)} %get-tuple-element.1182), channel_id=1, source_target_pairs={{0,256},{1,257},{2,258},{3,259},{4,260},{5,261},{6,262},{7,263},{8... | collective-permute-start | bytes 393224 | tf_op jit(solution)/shard_map/while/body/eval_jaxpr/ppermute | solution.py:15
  122.1 45.7 %collective-permute-start.1 = (bf16[2,8,8,512]{3,2,1,0:T(8,128)(2,1)}, bf16[2,8,8,512]{3,2,1,0:T(8,128)(2,1)S(1)}, u32[]{:S(2)}, u32[]{:S(2)}) collective-permute-start(bf16[2,8,8,512]{3,2,1,0:T(8,128)(2,1)} %get-tuple-element.1027), channel_id=1, source_target_pairs={{256,0},{257,1},{258,2},{259,3},{260,4},{261,5},{262,6},{263,7},{2... | collective-permute-start | bytes 393224 | tf_op jit(solution)/shard_map/while/body/eval_jaxpr/ppermute | solution.py:15
  128.8 39.1 %copy-start.5 = (f32[4,9,512]{2,1,0:T(8,128)}, f32[4,9,512]{2,1,0:T(8,128)S(1)}, u32[]{:S(2)}) copy-start(f32[4,9,512]{2,1,0:T(8,128)S(1)} %select_add_fusion.7) | copy-start | bytes 221188 | tf_op jit(solution)/shard_map/while
  129.6 38.3 %copy-start.8 = (f32[4,512]{1,0:T(4,128)}, f32[4,512]{1,0:T(4,128)S(1)}, u32[]{:S(2)}) copy-start(f32[4,512]{1,0:T(4,128)S(1)} %select_add_fusion.8) | copy-start | bytes 24580 | tf_op jit(solution)/shard_map/while
  182.8 7.9 copy-start.13
  195.6 29.9 %collective-permute-start.1 = (bf16[2,8,8,512]{3,2,1,0:T(8,128)(2,1)}, bf16[2,8,8,512]{3,2,1,0:T(8,128)(2,1)S(1)}, u32[]{:S(2)}, u32[]{:S(2)}) collective-permute-start(bf16[2,8,8,512]{3,2,1,0:T(8,128)(2,1)} %get-tuple-element.1027), channel_id=1, source_target_pairs={{256,0},{257,1},{258,2},{259,3},{260,4},{261,5},{262,6},{263,7},{2... | collective-permute-start | bytes 393224 | tf_op jit(solution)/shard_map/while/body/eval_jaxpr/ppermute | solution.py:15
  203.5 21.9 %copy-start.5 = (f32[4,9,512]{2,1,0:T(8,128)}, f32[4,9,512]{2,1,0:T(8,128)S(1)}, u32[]{:S(2)}) copy-start(f32[4,9,512]{2,1,0:T(8,128)S(1)} %select_add_fusion.7) | copy-start | bytes 221188 | tf_op jit(solution)/shard_map/while
  204.3 21.2 %copy-start.8 = (f32[4,512]{1,0:T(4,128)}, f32[4,512]{1,0:T(4,128)S(1)}, u32[]{:S(2)}) copy-start(f32[4,512]{1,0:T(4,128)S(1)} %select_add_fusion.8) | copy-start | bytes 24580 | tf_op jit(solution)/shard_map/while
  240.3 7.9 copy-start.11
  240.3 7.9 copy-start.13
  253.1 31.1 %collective-permute-start.1 = (bf16[2,8,8,512]{3,2,1,0:T(8,128)(2,1)}, bf16[2,8,8,512]{3,2,1,0:T(8,128)(2,1)S(1)}, u32[]{:S(2)}, u32[]{:S(2)}) collective-permute-start(bf16[2,8,8,512]{3,2,1,0:T(8,128)(2,1)} %get-tuple-element.1027), channel_id=1, source_target_pairs={{256,0},{257,1},{258,2},{259,3},{260,4},{261,5},{262,6},{263,7},{2... | collective-permute-start | bytes 393224 | tf_op jit(solution)/shard_map/while/body/eval_jaxpr/ppermute | solution.py:15
  261.0 23.2 %copy-start.5 = (f32[4,9,512]{2,1,0:T(8,128)}, f32[4,9,512]{2,1,0:T(8,128)S(1)}, u32[]{:S(2)}) copy-start(f32[4,9,512]{2,1,0:T(8,128)S(1)} %select_add_fusion.7) | copy-start | bytes 221188 | tf_op jit(solution)/shard_map/while
  261.8 22.4 %copy-start.8 = (f32[4,512]{1,0:T(4,128)}, f32[4,512]{1,0:T(4,128)S(1)}, u32[]{:S(2)}) copy-start(f32[4,512]{1,0:T(4,128)S(1)} %select_add_fusion.8) | copy-start | bytes 24580 | tf_op jit(solution)/shard_map/while
  299.2 7.9 copy-start.13
  311.9 31.1 %collective-permute-start.1 = (bf16[2,8,8,512]{3,2,1,0:T(8,128)(2,1)}, bf16[2,8,8,512]{3,2,1,0:T(8,128)(2,1)S(1)}, u32[]{:S(2)}, u32[]{:S(2)}) collective-permute-start(bf16[2,8,8,512]{3,2,1,0:T(8,128)(2,1)} %get-tuple-element.1027), channel_id=1, source_target_pairs={{256,0},{257,1},{258,2},{259,3},{260,4},{261,5},{262,6},{263,7},{2... | collective-permute-start | bytes 393224 | tf_op jit(solution)/shard_map/while/body/eval_jaxpr/ppermute | solution.py:15
  319.9 23.2 %copy-start.5 = (f32[4,9,512]{2,1,0:T(8,128)}, f32[4,9,512]{2,1,0:T(8,128)S(1)}, u32[]{:S(2)}) copy-start(f32[4,9,512]{2,1,0:T(8,128)S(1)} %select_add_fusion.7) | copy-start | bytes 221188 | tf_op jit(solution)/shard_map/while
  320.6 22.4 %copy-start.8 = (f32[4,512]{1,0:T(4,128)}, f32[4,512]{1,0:T(4,128)S(1)}, u32[]{:S(2)}) copy-start(f32[4,512]{1,0:T(4,128)S(1)} %select_add_fusion.8) | copy-start | bytes 24580 | tf_op jit(solution)/shard_map/while
  358.0 7.9 copy-start.13
  370.8 8.7 collective-permute-start.1
  (33 other events, 111.7 us)
Sparse Core Ops, SparseCore 0:
  381.8 251.9 all-reduce.17
where the time goes:
time: 1100 us
  blocking collectives  701 us (64%)
  waiting for transfers between devices  109 us (10%)
  other arithmetic  85.8 us (8%)
  local copies, waits for them, and re-layouts  65.5 us (6%)
  starting transfers between devices  63.4 us (6%)
  loops' own time  29.5 us (3%)
  matrix products  26.4 us (2%)
  between operations  14.1 us (1%)
    psum x1, blocking collectives, local(): lax.psum((point_acc, depth_acc, gain_acc), 'dp')  701 us
    ppermute x10, waiting for transfers between devices, passed_along(): return lax.ppermute(block, axis, route)  109 us
    ppermute x10, starting transfers between devices, passed_along(): return lax.ppermute(block, axis, route)  63.3 us
    add x5, other arithmetic, backward_step(): point_run + point_term  31.5 us
  transfers between devices with their start and end apart: 11, of which 9 were waited for; matrix products, arithmetic and copies ran while one was open for 3% of the time, Pallas kernels for 0%

commit v1 on v0

v1 whole, which is shorter than its diff:
```python
import jax
import jax.numpy as jnp
from jax import lax
from jax.experimental import pallas as pl
from jax.experimental.pallas import tpu as pltpu
from jax.sharding import Mesh, PartitionSpec as P

EPSILON = 1e-06
f32, bf16 = jnp.float32, jnp.bfloat16
LANES = 128


def cells_kernel(
    counts, where_, images, cotangent, vec_own, vec_far, point_own, point_far,
    kept, sent,
    point, vec, folded, state, normed, inverse, slope, act, grad_run, grad_act, mixed, taps, sems,
):
    half, channels = point_own.shape[0], point_own.shape[2]
    slots = 2 * half
    groups, height, width = images.shape[0], images.shape[2], images.shape[3]
    pixels = height * width
    tiles = channels // LANES
    mine = where_[0] * half
    theirs = half - mine
    copies = [
        pltpu.make_async_copy(point_own, point.at[pl.ds(mine, half)], sems.at[0]),
        pltpu.make_async_copy(point_far, point.at[pl.ds(theirs, half)], sems.at[1]),
    ]
    for copy in copies:
        copy.start()
    vec[pl.ds(mine, half)] = vec_own[...]
    vec[pl.ds(theirs, half)] = vec_far[...]
    for m in range(groups):
        state[m * pixels:(m + 1) * pixels] = images[m, 0].reshape(pixels, channels).astype(f32)
        grad_run[m * pixels:(m + 1) * pixels] = cotangent[m, 0].reshape(pixels, channels).astype(f32)
    for copy in copies:
        copy.wait()

    column = lax.broadcasted_iota(jnp.int32, (width, LANES), 0)
    not_first = column > 0
    not_last = column < width - 1

    def from_left(a):
        return jnp.where(not_first, pltpu.roll(a, 1, 0), 0.0)

    def from_right(a):
        return jnp.where(not_last, pltpu.roll(a, width - 1, 0), 0.0)

    def rows_of(block):
        return [block[h * width:(h + 1) * width] for h in range(height)]

    def active(k):
        return lax.rem(k, half) < counts[lax.div(k, half)]

    def forward(k, carry):
        @pl.when(active(k))
        def _():
            gain = vec[k, 9:10, :]
            for t in range(9):
                folded[k, t:t + 1, :] = vec[k, t:t + 1, :] * gain

            def image(m, c):
                rows = pl.ds(pl.multiple_of(m * pixels, pixels), pixels)
                x = state[rows, :]
                inv = lax.rsqrt(jnp.mean(x * x, axis=-1, keepdims=True) + EPSILON)
                inverse[k, rows, :] = jnp.broadcast_to(inv, (pixels, LANES))
                for j in range(tiles):
                    cs = slice(j * LANES, (j + 1) * LANES)
                    xn = x[:, cs] * inv
                    normed[k, rows, cs] = xn
                    mid = rows_of(xn)
                    left = [from_left(a) for a in mid]
                    right = [from_right(a) for a in mid]
                    w = [jnp.broadcast_to(folded[k, t:t + 1, cs], (width, LANES)) for t in range(9)]
                    acts, slopes = [], []
                    for h in range(height):
                        lin = None
                        for p in range(3):
                            r = h + p - 1
                            if r < 0 or r >= height:
                                continue
                            for q, src in enumerate((left, mid, right)):
                                term = w[p * 3 + q] * src[r]
                                lin = term if lin is None else lin + term
                        sig = 0.5 * jnp.tanh(0.5 * lin) + 0.5
                        a = lin * sig
                        acts.append(a)
                        slopes.append(sig + a * (1.0 - sig))
                    act[k, rows, cs] = jnp.concatenate(acts, axis=0).astype(bf16)
                    slope[k, rows, cs] = jnp.concatenate(slopes, axis=0)
                return c

            lax.fori_loop(0, groups, image, 0)
            mixed[...] = jnp.dot(act[k], point[k], preferred_element_type=f32)
            state[...] = (state[...] + mixed[...]).astype(bf16).astype(f32)
        return carry

    lax.fori_loop(0, slots, forward, 0)

    def backward(i, carry):
        k = slots - 1 - i

        home = lax.div(k, half) == where_[0]
        cell = lax.rem(k, half)

        def store(rows, value):
            @pl.when(home)
            def _():
                kept[cell, rows, :] = value

            @pl.when(jnp.logical_not(home))
            def _():
                sent[cell, rows, :] = value

        @pl.when(jnp.logical_not(active(k)))
        def _():
            store(slice(0, channels + 16), jnp.zeros((channels + 16, channels), bf16))

        @pl.when(active(k))
        def _():
            g = grad_run[...].astype(bf16)
            grad_act[...] = lax.dot_general(g, point[k], (((1,), (1,)), ((), ())), preferred_element_type=f32)
            store(
                slice(0, channels),
                lax.dot_general(act[k], g, (((0,), (0,)), ((), ())), preferred_element_type=f32).astype(bf16),
            )
            taps[...] = jnp.zeros_like(taps)

            def image(m, c):
                rows = pl.ds(pl.multiple_of(m * pixels, pixels), pixels)
                total = jnp.zeros((pixels, LANES), f32)
                for j in range(tiles):
                    cs = slice(j * LANES, (j + 1) * LANES)
                    gl = grad_act[rows, cs] * slope[k, rows, cs]
                    xn = normed[k, rows, cs]
                    mid = rows_of(gl)
                    src = ([from_right(a) for a in mid], mid, [from_left(a) for a in mid])
                    xr = rows_of(xn)
                    w = [jnp.broadcast_to(folded[k, t:t + 1, cs], (width, LANES)) for t in range(9)]
                    us = []
                    for h in range(height):
                        u = None
                        for p in range(3):
                            r = h - p + 1
                            if r < 0 or r >= height:
                                continue
                            for q in range(3):
                                term = w[p * 3 + q] * src[q][r]
                                u = term if u is None else u + term
                        us.append(u)
                    for p in range(3):
                        for q in range(3):
                            t = p * 3 + q
                            s = None
                            for h in range(height):
                                r = h - p + 1
                                if r < 0 or r >= height:
                                    continue
                                term = xr[h] * src[q][r]
                                s = term if s is None else s + term
                            taps[t * 8:(t + 1) * 8, cs] += s
                    u = jnp.concatenate(us, axis=0)
                    mixed[rows, cs] = u
                    total = total + u * xn
                mean = jnp.sum(total, axis=-1, keepdims=True) * (1.0 / channels)
                inv = inverse[k, rows, :]
                mean_b = jnp.broadcast_to(mean, (pixels, LANES))
                for j in range(tiles):
                    cs = slice(j * LANES, (j + 1) * LANES)
                    gx = grad_run[rows, cs] + inv * (mixed[rows, cs] - normed[k, rows, cs] * mean_b)
                    grad_run[rows, cs] = gx.astype(bf16).astype(f32)
                return c

            lax.fori_loop(0, groups, image, 0)
            gain = vec[k, 9:10, :]
            grad_gain = jnp.zeros((1, channels), f32)
            parts = []
            for t in range(9):
                summed = jnp.sum(taps[t * 8:(t + 1) * 8, :], axis=0, keepdims=True)
                parts.append(summed * gain)
                grad_gain = grad_gain + vec[k, t:t + 1, :] * summed
            parts += [grad_gain, jnp.zeros((6, channels), f32)]
            store(slice(channels, channels + 16), jnp.concatenate(parts, axis=0).astype(bf16))
        return carry

    lax.fori_loop(0, slots, backward, 0)


def run_cells(counts, section, images, cotangent, vec_own, vec_far, point_own, point_far):
    slots = 2 * point_own.shape[0]
    groups, unused, height, width, channels = images.shape
    total = groups * height * width
    share = (groups, 1, height, width, channels)
    vec_shape = (slots, 10, channels)
    packed = (slots // 2, channels + 16, channels)
    spec = pltpu.PrefetchScalarGridSpec(
        num_scalar_prefetch=2,
        grid=(1,),
        in_specs=[
            pl.BlockSpec(share, lambda i, c, s: (0, s[0], 0, 0, 0)),
            pl.BlockSpec(share, lambda i, c, s: (0, s[0], 0, 0, 0)),
            pl.BlockSpec(vec_own.shape, lambda i, c, s: (0, 0, 0)),
            pl.BlockSpec(vec_far.shape, lambda i, c, s: (0, 0, 0)),
            pl.BlockSpec(memory_space=pl.ANY),
            pl.BlockSpec(memory_space=pl.ANY),
        ],
        out_specs=[
            pl.BlockSpec(packed, lambda i, c, s: (0, 0, 0)),
            pl.BlockSpec(packed, lambda i, c, s: (0, 0, 0)),
        ],
        scratch_shapes=[
            pltpu.VMEM((slots, channels, channels), bf16),
            pltpu.VMEM(vec_shape, f32),
            pltpu.VMEM((slots, 9, channels), f32),
            pltpu.VMEM((total, channels), f32),
            pltpu.VMEM((slots, total, channels), f32),
            pltpu.VMEM((slots, total, LANES), f32),
            pltpu.VMEM((slots, total, channels), f32),
            pltpu.VMEM((slots, total, channels), bf16),
            pltpu.VMEM((total, channels), f32),
            pltpu.VMEM((total, channels), f32),
            pltpu.VMEM((total, channels), f32),
            pltpu.VMEM((72, channels), f32),
            pltpu.SemaphoreType.DMA((2,)),
        ],
    )
    return pl.pallas_call(
        cells_kernel,
        grid_spec=spec,
        out_shape=[
            jax.ShapeDtypeStruct(packed, bf16),
            jax.ShapeDtypeStruct(packed, bf16),
        ],
        compiler_params=pltpu.CompilerParams(vmem_limit_bytes=56 << 20),
        name="cells",
    )(counts, section, images, cotangent, vec_own, vec_far, point_own, point_far)


def swapped(block):
    return lax.ppermute(block, "section", [(0, 1), (1, 0)])


def local(images, cotangent, counts, gains, depthwise, pointwise):
    cells, channels = gains.shape
    section = lax.axis_index("section").astype(jnp.int32)
    vec_own = jnp.concatenate([depthwise, gains[:, None, :]], axis=1)
    counts_far = swapped(counts)
    both = jnp.where(section == 0, jnp.concatenate([counts, counts_far]), jnp.concatenate([counts_far, counts]))
    kept, sent = run_cells(
        both, section[None], images, cotangent, vec_own, swapped(vec_own), pointwise, swapped(pointwise)
    )
    summed = (kept.astype(f32) + swapped(sent).astype(f32)).astype(bf16)

    along = lax.axis_size("x")
    plane = lax.axis_size("z") * lax.axis_size("y")
    parts = lax.all_to_all(summed, "x", 0, 0, tiled=True)
    cell = jnp.sum(parts.astype(f32).reshape((along,) + summed.shape[1:]), axis=0)
    point, vec = cell[:channels], cell[channels:channels + 16]
    strip = jnp.pad(vec.reshape(-1, LANES), ((0, channels - vec.size // LANES), (0, 0)))
    wide = jnp.concatenate([point, strip], axis=1).astype(bf16).reshape(plane, channels // plane, channels + LANES)
    piece = jnp.sum(lax.all_to_all(wide, ("z", "y"), 0, 0, tiled=True).astype(f32), axis=0).astype(bf16)

    whole = lax.all_to_all(jnp.broadcast_to(piece, wide.shape), ("z", "y"), 0, 0, tiled=True)
    whole = whole.reshape(1, channels, channels + LANES)
    whole = lax.all_to_all(jnp.broadcast_to(whole, (along,) + whole.shape[1:]), "x", 0, 0, tiled=True)
    out = whole.astype(f32)
    small = out[:, :16 * channels // LANES, channels:].reshape(cells, 16, channels)
    return out[:, :, :channels], small[:, :9], small[:, 9]


def solution(mesh):
    grid = Mesh(mesh.devices.reshape(2, 8, 8, 4), ("section", "z", "y", "x"))
    data = ("z", "y", "x")
    placed = (
        P(None, data, None, None, None),
        P(None, data, None, None, None),
        P("section"),
        P("section", None),
        P("section", None, None),
        P("section", None, None),
    )
    return jax.shard_map(
        local,
        mesh=grid,
        in_specs=placed,
        out_specs=(P("section", None, None), P("section", None, None), P("section", None)),
        check_vma=False,
    )
```

time: 1100 us -> 177 us (0.16)
  the two profiles are of different devices: /device:TPU:0 before, /device:TPU:16 now
where the time goes in v1:
time: 177 us; the launch traced here: 176 us
  blocking collectives  126 us (71%)
  Pallas kernels  24.7 us (14%)
  starting transfers between devices  8.63 us (5%)
  local copies, waits for them, and re-layouts  7.18 us (4%)
  other arithmetic  4.3 us (2%)
  waiting for transfers between devices  4.08 us (2%)
    all_to_all x1, blocking collectives, local(): lax.all_to_all(wide, ('z', 'y'), 0, 0, tiled=True).astype(f32)  37 us
    all_to_all x1, blocking collectives, local(): parts = lax.all_to_all(summed, 'x', 0, 0, tiled=True)  31.7 us
    all_to_all x1, blocking collectives, local(): lax.all_to_all(jnp.broadcast_to(whole, (along,) + whole.shape[1:]), 'x',...  31.4 us
    all_to_all x1, blocking collectives, local(): lax.all_to_all(jnp.broadcast_to(piece, wide.shape), ('z', 'y'), 0, 0, til...  25.9 us
    pallas_call x1, Pallas kernels, run_cells(): pl.pallas_call(cells_kernel, grid_spec=spec, out_shape=[jax.ShapeDtypeStr...  24.7 us
    ppermute x4, starting transfers between devices, swapped(): return lax.ppermute(block, 'section', [(0, 1), (1, 0)])  8.63 us
    ppermute x4, waiting for transfers between devices, swapped(): return lax.ppermute(block, 'section', [(0, 1), (1, 0)])  4.08 us
  transfers between devices with their start and end apart: 4, of which 1 were waited for; matrix products, arithmetic and copies ran while one was open for 2% of the time, Pallas kernels for 0%

profile of v1, /device:TPU:16, one launch (start us, length us, event | category | flops | bytes accessed | tf_op | source)
XLA Modules:
  0.0 176.3 jit_solution(12019896215562554817)
XLA Ops:
  0.6 1.9 %collective-permute-start.2 = (bf16[4,512,512]{2,1,0:T(8,128)(2,1)}, bf16[4,512,512]{2,1,0:T(8,128)(2,1)S(1)}, u32[]{:S(2)}, u32[]{:S(2)}) collective-permute-start(bf16[4,512,512]{2,1,0:T(8,128)(2,1)} %point_own.1), channel_id=1, source_target_pairs={{0,256},{256,0},{1,257},{257,1},{2,258},{258,2},{3,259},{259,3},{4... | collective-permute-start | bytes 6291464 | tf_op jit(solution)/shard_map/ppermute | solution.py:240
  2.6 2.4 %collective-permute-start = (s32[1]{0:T(128)}, s32[1]{0:T(128)}, u32[]{:S(2)}, u32[]{:S(2)}) collective-permute-start(s32[1]{0:T(128)} %param.8), channel_id=1, source_target_pairs={{0,256},{256,0},{1,257},{257,1},{2,258},{258,2},{3,259},{259,3},{4... | collective-permute-start | bytes 20 | tf_op jit(solution)/shard_map/ppermute | solution.py:240
  5.0 0.7 broadcast_in_dim.17
  5.7 0.9 copy.12
  6.6 1.9 %collective-permute-start.1 = (f32[4,10,512]{2,1,0:T(8,128)S(1)}, f32[4,10,512]{2,1,0:T(8,128)S(1)}, u32[]{:S(2)}, u32[]{:S(2)}) collective-permute-start(f32[4,10,512]{2,1,0:T(8,128)S(1)} %pad_maximum_fusion.1.vec_own), channel_id=1, source_target_pairs={{0,256},{256,0},{1,257},{257,1},{2,258},{258,2},{3,259},{259,3},{4... | collective-permute-start | bytes 245768 | tf_op jit(solution)/shard_map/ppermute | solution.py:240
  9.2 1.2 broadcast_select_fusion.counts
  10.5 0.6 copy-done.2
  11.1 0.7 copy-done
  11.8 24.7 %cells.1 = (bf16[4,528,512]{2,1,0:T(8,128)(2,1)}, bf16[4,528,512]{2,1,0:T(8,128)(2,1)}) custom-call(s32[2]{0:T(128)} %broadcast_select_fusion.counts, s32[1]{0:T(128)} %bitcast.where_, bf16[4,2,8,8,512]{4,3,2,1,0:T(8,128)(2,1)} %images.1, bf16[4,2,8,8,512]{4,3,2,1,0:T(8,128)(2,1)} %cotangent.1, f32[4,10,512]{2,1,0:T(8,128)} %copy-done.1, ...), custom_call_target="tpu_custom_call" | custom-call | tf_op jit(solution)/shard_map/cells/pallas_call | solution.py:227
  36.5 2.4 %collective-permute-start.3 = (bf16[4,528,512]{2,1,0:T(8,128)(2,1)}, bf16[4,528,512]{2,1,0:T(8,128)(2,1)S(1)}, u32[]{:S(2)}, u32[]{:S(2)}) collective-permute-start(bf16[4,528,512]{2,1,0:T(8,128)(2,1)} %get-tuple-element.6), channel_id=1, source_target_pairs={{0,256},{256,0},{1,257},{257,1},{2,258},{258,2},{3,259},{259,3},{4... | collective-permute-start | bytes 6488072 | tf_op jit(solution)/shard_map/ppermute | solution.py:240
  38.9 4.1 %collective-permute-done.3 = bf16[4,528,512]{2,1,0:T(8,128)(2,1)S(1)} collective-permute-done((bf16[4,528,512]{2,1,0:T(8,128)(2,1)}, bf16[4,528,512]{2,1,0:T(8,128)(2,1)S(1)}, u32[]{:S(2)}, u32[]{:S(2)}) %collective-permute-start.3) | collective-permute-done | bytes 2162720 | tf_op jit(solution)/shard_map/ppermute | solution.py:240
  42.9 2.2 %add_convert_fusion = bf16[4,528,512]{2,1,0:T(8,128)(2,1)S(1)} fusion(bf16[4,528,512]{2,1,0:T(8,128)(2,1)S(1)} %collective-permute-done.3, bf16[4,528,512]{2,1,0:T(8,128)(2,1)} %get-tuple-element.5), kind=kLoop, calls=%fused_computation | loop fusion | flops 4325376 | bytes 6488064 | tf_op jit(solution)/shard_map/convert_element_type | solution.py:252
  45.2 31.7 %all_to_all.20 = bf16[4,528,512]{2,1,0:T(8,128)(2,1)S(1)} all-to-all(bf16[4,528,512]{2,1,0:T(8,128)(2,1)S(1)} %add_convert_fusion), channel_id=1, replica_groups=mesh['section'=2,'z'=8,'y'=8,'x'=4] {'x'}, dimensions={0} | all-to-all | bytes 4325376 | tf_op jit(solution)/shard_map/all_to_all | solution.py:256
  76.8 0.7 reduce.1
  77.6 0.1 pad_maximum_fusion
  77.7 37.0 %all_to_all.21 = bf16[64,8,640]{2,1,0:T(8,128)(2,1)S(1)} all-to-all(bf16[64,8,640]{2,1,0:T(8,128)(2,1)S(1)} %pad_maximum_fusion), channel_id=1, replica_groups=mesh['section'=2,'z'=8,'y'=8,'x'=4] {'z','y'}, dimensions={0} | all-to-all | bytes 1310720 | tf_op jit(solution)/shard_map/all_to_all | solution.py:261
  114.7 0.1 reduce_sum.22
  114.8 0.1 broadcast_in_dim.18
  114.9 25.9 %all_to_all.22 = bf16[64,8,640]{2,1,0:T(8,128)(2,1)S(1)} all-to-all(bf16[64,8,640]{2,1,0:T(8,128)(2,1)S(1)} %broadcast_in_dim.18), channel_id=1, replica_groups=mesh['section'=2,'z'=8,'y'=8,'x'=4] {'z','y'}, dimensions={0} | all-to-all | bytes 1310720 | tf_op jit(solution)/shard_map/all_to_all | solution.py:263
  140.8 0.2 broadcast_in_dim.20
  141.0 31.4 %all_to_all.23 = bf16[4,512,640]{2,1,0:T(8,128)(2,1)S(1)} all-to-all(bf16[4,512,640]{2,1,0:T(8,128)(2,1)S(1)} %broadcast_in_dim.20), channel_id=1, replica_groups=mesh['section'=2,'z'=8,'y'=8,'x'=4] {'x'}, dimensions={0} | all-to-all | bytes 5242880 | tf_op jit(solution)/shard_map/all_to_all | solution.py:265
  172.5 0.6 copy.16
  173.1 0.7 copy.13
  173.7 2.6 %slice.28 = f32[4,512,512]{2,1,0:T(8,128)} slice(bf16[4,512,640]{2,1,0:T(8,128)(2,1)S(1)} %all_to_all.23), slice={[0:4], [0:512], [0:512]} | slice | bytes 8388608 | tf_op jit(solution)/shard_map/slice | solution.py:268
  (15 shorter events, 0.1 us)
Async XLA Ops:
  0.6 9.8 %collective-permute-start.2 = (bf16[4,512,512]{2,1,0:T(8,128)(2,1)}, bf16[4,512,512]{2,1,0:T(8,128)(2,1)S(1)}, u32[]{:S(2)}, u32[]{:S(2)}) collective-permute-start(bf16[4,512,512]{2,1,0:T(8,128)(2,1)} %point_own.1), channel_id=1, source_target_pairs={{0,256},{256,0},{1,257},{257,1},{2,258},{258,2},{3,259},{259,3},{4... | collective-permute-start | bytes 6291464 | tf_op jit(solution)/shard_map/ppermute | solution.py:240
  2.6 6.7 %collective-permute-start = (s32[1]{0:T(128)}, s32[1]{0:T(128)}, u32[]{:S(2)}, u32[]{:S(2)}) collective-permute-start(s32[1]{0:T(128)} %param.8), channel_id=1, source_target_pairs={{0,256},{256,0},{1,257},{257,1},{2,258},{258,2},{3,259},{259,3},{4... | collective-permute-start | bytes 20 | tf_op jit(solution)/shard_map/ppermute | solution.py:240
  6.6 3.8 %copy-start.1 = (f32[4,10,512]{2,1,0:T(8,128)}, f32[4,10,512]{2,1,0:T(8,128)S(1)}, u32[]{:S(2)}) copy-start(f32[4,10,512]{2,1,0:T(8,128)S(1)} %pad_maximum_fusion.1.vec_own) | copy-start | bytes 245764
  6.6 3.8 %collective-permute-start.1 = (f32[4,10,512]{2,1,0:T(8,128)S(1)}, f32[4,10,512]{2,1,0:T(8,128)S(1)}, u32[]{:S(2)}, u32[]{:S(2)}) collective-permute-start(f32[4,10,512]{2,1,0:T(8,128)S(1)} %pad_maximum_fusion.1.vec_own), channel_id=1, source_target_pairs={{0,256},{256,0},{1,257},{257,1},{2,258},{258,2},{3,259},{259,3},{4... | collective-permute-start | bytes 245768 | tf_op jit(solution)/shard_map/ppermute | solution.py:240
  10.4 0.7 copy-start.2
  10.5 1.3 copy-start
  36.5 6.5 %collective-permute-start.3 = (bf16[4,528,512]{2,1,0:T(8,128)(2,1)}, bf16[4,528,512]{2,1,0:T(8,128)(2,1)S(1)}, u32[]{:S(2)}, u32[]{:S(2)}) collective-permute-start(bf16[4,528,512]{2,1,0:T(8,128)(2,1)} %get-tuple-element.6), channel_id=1, source_target_pairs={{0,256},{256,0},{1,257},{257,1},{2,258},{258,2},{3,259},{259,3},{4... | collective-permute-start | bytes 6488072 | tf_op jit(solution)/shard_map/ppermute | solution.py:240

commit v2 on v1

--- a/solution.py
+++ b/solution.py
@@ -8,14 +8,19 @@
 EPSILON = 1e-06
 f32, bf16 = jnp.float32, jnp.bfloat16
 LANES = 128
+QUARTERS = 4
+NEAR = ("zl", "yl", "x")
+FAR = ("zh", "yh")
 
 
 def cells_kernel(
-    counts, where_, images, cotangent, vec_own, vec_far, point_own, point_far,
+    where_, images, cotangent, vec_own, vec_far, point_own, point_far,
     kept, sent,
     point, vec, folded, state, normed, inverse, slope, act, grad_run, grad_act, mixed, taps, sems,
 ):
     half, channels = point_own.shape[0], point_own.shape[2]
+    quarters = kept.shape[0] // half
+    block = channels // quarters
     slots = 2 * half
     groups, height, width = images.shape[0], images.shape[2], images.shape[3]
     pixels = height * width
@@ -33,9 +38,6 @@
     for m in range(groups):
         state[m * pixels:(m + 1) * pixels] = images[m, 0].reshape(pixels, channels).astype(f32)
         grad_run[m * pixels:(m + 1) * pixels] = cotangent[m, 0].reshape(pixels, channels).astype(f32)
-    for copy in copies:
-        copy.wait()
-
     column = lax.broadcasted_iota(jnp.int32, (width, LANES), 0)
     not_first = column > 0
     not_last = column < width - 1
@@ -49,8 +51,12 @@
     def rows_of(block):
         return [block[h * width:(h + 1) * width] for h in range(height)]
 
+    count_own = jnp.max(vec_own[0, 10:11, :])
+    count_far = jnp.max(vec_far[0, 10:11, :])
+
     def active(k):
-        return lax.rem(k, half) < counts[lax.div(k, half)]
+        limit = jnp.where(lax.div(k, half) == where_[0], count_own, count_far)
+        return lax.rem(k, half).astype(f32) < limit
 
     def forward(k, carry):
         @pl.when(active(k))
@@ -91,6 +97,14 @@
                 return c
 
             lax.fori_loop(0, groups, image, 0)
+
+        @pl.when(k == 0)
+        def _():
+            for copy in copies:
+                copy.wait()
+
+        @pl.when(active(k))
+        def _():
             mixed[...] = jnp.dot(act[k], point[k], preferred_element_type=f32)
             state[...] = (state[...] + mixed[...]).astype(bf16).astype(f32)
         return carry
@@ -103,25 +117,31 @@
         home = lax.div(k, half) == where_[0]
         cell = lax.rem(k, half)
 
-        def store(rows, value):
+        def store(first, count, value):
+            rows = slice(first, first + count)
+
             @pl.when(home)
             def _():
-                kept[cell, rows, :] = value
+                for r in range(quarters):
+                    kept[quarters * cell + r, rows, :] = value[r * count:(r + 1) * count]
 
             @pl.when(jnp.logical_not(home))
             def _():
-                sent[cell, rows, :] = value
+                for r in range(quarters):
+                    sent[quarters * cell + r, rows, :] = value[r * count:(r + 1) * count]
 
         @pl.when(jnp.logical_not(active(k)))
         def _():
-            store(slice(0, channels + 16), jnp.zeros((channels + 16, channels), bf16))
+            store(0, block, jnp.zeros((channels, channels), bf16))
+            store(block, 8, jnp.zeros((quarters * 8, channels), bf16))
 
         @pl.when(active(k))
         def _():
             g = grad_run[...].astype(bf16)
             grad_act[...] = lax.dot_general(g, point[k], (((1,), (1,)), ((), ())), preferred_element_type=f32)
             store(
-                slice(0, channels),
+                0,
+                block,
                 lax.dot_general(act[k], g, (((0,), (0,)), ((), ())), preferred_element_type=f32).astype(bf16),
             )
             taps[...] = jnp.zeros_like(taps)
@@ -179,34 +199,37 @@
                 summed = jnp.sum(taps[t * 8:(t + 1) * 8, :], axis=0, keepdims=True)
                 parts.append(summed * gain)
                 grad_gain = grad_gain + vec[k, t:t + 1, :] * summed
-            parts += [grad_gain, jnp.zeros((6, channels), f32)]
-            store(slice(channels, channels + 16), jnp.concatenate(parts, axis=0).astype(bf16))
+            parts += [grad_gain, jnp.zeros((2, channels), f32)]
+            spread = []
+            for r in range(quarters):
+                spread += parts[r * 3:r * 3 + 3] + [jnp.zeros((5, channels), f32)]
+            store(block, 8, jnp.concatenate(spread[:15] + [jnp.zeros((7, channels), f32)], axis=0).astype(bf16))
         return carry
 
     lax.fori_loop(0, slots, backward, 0)
 
 
-def run_cells(counts, section, images, cotangent, vec_own, vec_far, point_own, point_far):
+def run_cells(section, images, cotangent, vec_own, vec_far, point_own, point_far):
     slots = 2 * point_own.shape[0]
     groups, unused, height, width, channels = images.shape
     total = groups * height * width
     share = (groups, 1, height, width, channels)
-    vec_shape = (slots, 10, channels)
-    packed = (slots // 2, channels + 16, channels)
+    vec_shape = (slots, 11, channels)
+    packed = (QUARTERS * slots // 2, channels // QUARTERS + 8, channels)
     spec = pltpu.PrefetchScalarGridSpec(
-        num_scalar_prefetch=2,
+        num_scalar_prefetch=1,
         grid=(1,),
         in_specs=[
-            pl.BlockSpec(share, lambda i, c, s: (0, s[0], 0, 0, 0)),
-            pl.BlockSpec(share, lambda i, c, s: (0, s[0], 0, 0, 0)),
-            pl.BlockSpec(vec_own.shape, lambda i, c, s: (0, 0, 0)),
-            pl.BlockSpec(vec_far.shape, lambda i, c, s: (0, 0, 0)),
+            pl.BlockSpec(share, lambda i, s: (0, s[0], 0, 0, 0)),
+            pl.BlockSpec(share, lambda i, s: (0, s[0], 0, 0, 0)),
+            pl.BlockSpec(vec_own.shape, lambda i, s: (0, 0, 0)),
+            pl.BlockSpec(vec_far.shape, lambda i, s: (0, 0, 0)),
             pl.BlockSpec(memory_space=pl.ANY),
             pl.BlockSpec(memory_space=pl.ANY),
         ],
         out_specs=[
-            pl.BlockSpec(packed, lambda i, c, s: (0, 0, 0)),
-            pl.BlockSpec(packed, lambda i, c, s: (0, 0, 0)),
+            pl.BlockSpec(packed, lambda i, s: (0, 0, 0)),
+            pl.BlockSpec(packed, lambda i, s: (0, 0, 0)),
         ],
         scratch_shapes=[
             pltpu.VMEM((slots, channels, channels), bf16),
@@ -233,44 +256,53 @@
         ],
         compiler_params=pltpu.CompilerParams(vmem_limit_bytes=56 << 20),
         name="cells",
-    )(counts, section, images, cotangent, vec_own, vec_far, point_own, point_far)
+    )(section, images, cotangent, vec_own, vec_far, point_own, point_far)
 
 
 def swapped(block):
     return lax.ppermute(block, "section", [(0, 1), (1, 0)])
+
+
+def exchanged(block, axes):
+    return lax.all_to_all(block, axes, 0, 0, tiled=True)
+
+
+def added(blocks):
+    return jnp.sum(blocks.astype(f32), axis=0)
 
 
 def local(images, cotangent, counts, gains, depthwise, pointwise):
     cells, channels = gains.shape
     section = lax.axis_index("section").astype(jnp.int32)
-    vec_own = jnp.concatenate([depthwise, gains[:, None, :]], axis=1)
-    counts_far = swapped(counts)
-    both = jnp.where(section == 0, jnp.concatenate([counts, counts_far]), jnp.concatenate([counts_far, counts]))
-    kept, sent = run_cells(
-        both, section[None], images, cotangent, vec_own, swapped(vec_own), pointwise, swapped(pointwise)
+    point_far = swapped(pointwise)
+    vec_own = jnp.concatenate(
+        [depthwise, gains[:, None, :], jnp.broadcast_to(counts.astype(f32)[:, None, None], (cells, 1, channels))],
+        axis=1,
     )
+    vec_far = swapped(vec_own)
+    kept, sent = run_cells(section[None], images, cotangent, vec_own, vec_far, pointwise, point_far)
     summed = (kept.astype(f32) + swapped(sent).astype(f32)).astype(bf16)
 
-    along = lax.axis_size("x")
-    plane = lax.axis_size("z") * lax.axis_size("y")
-    parts = lax.all_to_all(summed, "x", 0, 0, tiled=True)
-    cell = jnp.sum(parts.astype(f32).reshape((along,) + summed.shape[1:]), axis=0)
-    point, vec = cell[:channels], cell[channels:channels + 16]
-    strip = jnp.pad(vec.reshape(-1, LANES), ((0, channels - vec.size // LANES), (0, 0)))
-    wide = jnp.concatenate([point, strip], axis=1).astype(bf16).reshape(plane, channels // plane, channels + LANES)
-    piece = jnp.sum(lax.all_to_all(wide, ("z", "y"), 0, 0, tiled=True).astype(f32), axis=0).astype(bf16)
-
-    whole = lax.all_to_all(jnp.broadcast_to(piece, wide.shape), ("z", "y"), 0, 0, tiled=True)
-    whole = whole.reshape(1, channels, channels + LANES)
-    whole = lax.all_to_all(jnp.broadcast_to(whole, (along,) + whole.shape[1:]), "x", 0, 0, tiled=True)
-    out = whole.astype(f32)
-    small = out[:, :16 * channels // LANES, channels:].reshape(cells, 16, channels)
-    return out[:, :, :channels], small[:, :9], small[:, 9]
+    near, rows, unused = summed.shape
+    rows -= 8
+    far = lax.axis_size(FAR)
+    part = added(exchanged(summed, NEAR))
+    strip = part[rows:rows + 4].reshape(-1, LANES)
+    strip = jnp.pad(strip, ((0, rows - strip.shape[0]), (0, 0)))
+    wide = jnp.concatenate([part[:rows], strip], axis=1).astype(bf16).reshape(far, rows // far, channels + LANES)
+    piece = added(exchanged(wide, FAR)).astype(bf16)
+
+    back = exchanged(jnp.broadcast_to(piece, wide.shape), FAR).reshape(rows, channels + LANES)
+    small = back[:32, channels:].reshape(8, channels)
+    back = jnp.concatenate([back[:, :channels], small], axis=0)
+    out = exchanged(jnp.broadcast_to(back, summed.shape), NEAR).astype(f32)
+    small = out[:, rows:rows + 3].reshape(cells, 3 * QUARTERS, channels)
+    return out[:, :rows].reshape(cells, channels, channels), small[:, :9], small[:, 9]
 
 
 def solution(mesh):
-    grid = Mesh(mesh.devices.reshape(2, 8, 8, 4), ("section", "z", "y", "x"))
-    data = ("z", "y", "x")
+    grid = Mesh(mesh.devices.reshape(2, 4, 2, 4, 2, 4), ("section", "zh", "zl", "yh", "yl", "x"))
+    data = ("zh", "zl", "yh", "yl", "x")
     placed = (
         P(None, data, None, None, None),
         P(None, data, None, None, None),

time: 177 us -> 157 us (0.89)
  the two profiles are of different devices: /device:TPU:16 before, /device:TPU:2 now
where the time goes in v2:
time: 157 us; the launch traced here: 156 us
  blocking collectives  107 us (68%)
  Pallas kernels  25.8 us (16%)
  local copies, waits for them, and re-layouts  7.24 us (5%)
  starting transfers between devices  6.6 us (4%)
  waiting for transfers between devices  5.13 us (3%)
  other arithmetic  2.73 us (2%)
    all_to_all x4, blocking collectives, exchanged(): return lax.all_to_all(block, axes, 0, 0, tiled=True)  107 us
    pallas_call x1, Pallas kernels, run_cells(): pl.pallas_call(cells_kernel, grid_spec=spec, out_shape=[jax.ShapeDtypeStr...  25.8 us
    ppermute x3, starting transfers between devices, swapped(): return lax.ppermute(block, 'section', [(0, 1), (1, 0)])  6.6 us
    ppermute x3, waiting for transfers between devices, swapped(): return lax.ppermute(block, 'section', [(0, 1), (1, 0)])  5.13 us
    unnamed x9, local copies, waits for them, and re-layouts  3.54 us
  transfers between devices with their start and end apart: 3, of which 2 were waited for; matrix products, arithmetic and copies ran while one was open for 1% of the time, Pallas kernels for 0%

profile of v2, /device:TPU:2, one launch (start us, length us, event | category | flops | bytes accessed | tf_op | source)
XLA Modules:
  0.0 156.3 jit_solution(8206356042616782978)
XLA Ops:
  0.6 1.9 %collective-permute-start.1 = (bf16[4,512,512]{2,1,0:T(8,128)(2,1)}, bf16[4,512,512]{2,1,0:T(8,128)(2,1)S(1)}, u32[]{:S(2)}, u32[]{:S(2)}) collective-permute-start(bf16[4,512,512]{2,1,0:T(8,128)(2,1)} %point_own.1), channel_id=1, source_target_pairs={{0,256},{256,0},{1,257},{257,1},{2,258},{258,2},{3,259},{259,3},{4... | collective-permute-start | bytes 6291464 | tf_op jit(solution)/shard_map/ppermute | solution.py:263
  3.2 0.7 broadcast_in_dim.21
  3.9 0.9 copy.12
  4.8 0.1 pad.12.clone
  4.9 0.1 maximum_maximum_fusion.vec_own
  5.0 0.0 copy-start.1
  5.0 2.4 %collective-permute-start = (f32[4,11,512]{2,1,0:T(8,128)S(1)}, f32[4,11,512]{2,1,0:T(8,128)S(1)}, u32[]{:S(2)}, u32[]{:S(2)}) collective-permute-start(f32[4,11,512]{2,1,0:T(8,128)S(1)} %maximum_maximum_fusion.vec_own), channel_id=1, source_target_pairs={{0,256},{256,0},{1,257},{257,1},{2,258},{258,2},{3,259},{259,3},{4... | collective-permute-start | bytes 270344 | tf_op jit(solution)/shard_map/ppermute | solution.py:263
  7.4 1.0 collective-permute-done.vec_far
  8.4 0.0 collective-permute-done.1.point_far
  8.4 0.6 copy-done.2
  9.0 0.7 copy-done
  9.7 25.8 %cells.1 = (bf16[16,136,512]{2,1,0:T(8,128)(2,1)}, bf16[16,136,512]{2,1,0:T(8,128)(2,1)}) custom-call(s32[1]{0:T(128)} %bitcast.where_, bf16[4,2,8,8,512]{4,3,2,1,0:T(8,128)(2,1)} %images.1, bf16[4,2,8,8,512]{4,3,2,1,0:T(8,128)(2,1)} %cotangent.1, f32[4,11,512]{2,1,0:T(8,128)} %copy-done.1, f32[4,11,512]{2,1,0:T(8,128)} %copy-done.2, ...), custom_call_target="tpu_custom_call" | custom-call | tf_op jit(solution)/shard_map/cells/pallas_call | solution.py:250
  35.5 2.3 %collective-permute-start.2 = (bf16[16,136,512]{2,1,0:T(8,128)(2,1)}, bf16[16,136,512]{2,1,0:T(8,128)(2,1)S(1)}, u32[]{:S(2)}, u32[]{:S(2)}) collective-permute-start(bf16[16,136,512]{2,1,0:T(8,128)(2,1)} %get-tuple-element.6), channel_id=1, source_target_pairs={{0,256},{256,0},{1,257},{257,1},{2,258},{258,2},{3,259},{259,3},{4... | collective-permute-start | bytes 6684680 | tf_op jit(solution)/shard_map/ppermute | solution.py:263
  37.8 4.2 %collective-permute-done.2 = bf16[16,136,512]{2,1,0:T(8,128)(2,1)S(1)} collective-permute-done((bf16[16,136,512]{2,1,0:T(8,128)(2,1)}, bf16[16,136,512]{2,1,0:T(8,128)(2,1)S(1)}, u32[]{:S(2)}, u32[]{:S(2)}) %collective-permute-start.2) | collective-permute-done | bytes 2228256 | tf_op jit(solution)/shard_map/ppermute | solution.py:263
  42.0 2.3 %add_convert_fusion = bf16[16,136,512]{2,1,0:T(8,128)(2,1)S(1)} fusion(bf16[16,136,512]{2,1,0:T(8,128)(2,1)S(1)} %collective-permute-done.2, bf16[16,136,512]{2,1,0:T(8,128)(2,1)} %get-tuple-element.5), kind=kLoop, calls=%fused_computation | loop fusion | flops 4456448 | bytes 6684672 | tf_op jit(solution)/shard_map/convert_element_type | solution.py:284
  44.2 37.3 %all_to_all.20 = bf16[16,136,512]{2,1,0:T(8,128)(2,1)S(1)} all-to-all(bf16[16,136,512]{2,1,0:T(8,128)(2,1)S(1)} %add_convert_fusion), channel_id=1, replica_groups=mesh['section'=2,'zh'=4,'zl'=2,'yh'=4,'yl'=2,'x'=4] {'zl','yl','x'}, dimensions={0} | all-to-all | bytes 4456448 | tf_op jit(solution)/shard_map/all_to_all | solution.py:267
  81.5 0.3 reduce.1
  81.9 25.0 %all_to_all.21 = bf16[16,8,640]{2,1,0:T(8,128)(2,1)S(1)} all-to-all(bf16[16,8,640]{2,1,0:T(8,128)(2,1)S(1)} %pad_maximum_fusion), channel_id=1, replica_groups=mesh['section'=2,'zh'=4,'zl'=2,'yh'=4,'yl'=2,'x'=4] {'zh','yh'}, dimensions={0} | all-to-all | bytes 327680 | tf_op jit(solution)/shard_map/all_to_all | solution.py:267
  107.0 16.1 %all_to_all.22 = bf16[16,8,640]{2,1,0:T(8,128)(2,1)S(1)} all-to-all(bf16[16,8,640]{2,1,0:T(8,128)(2,1)S(1)} %broadcast_in_dim.24), channel_id=1, replica_groups=mesh['section'=2,'zh'=4,'zl'=2,'yh'=4,'yl'=2,'x'=4] {'zh','yh'}, dimensions={0} | all-to-all | bytes 327680 | tf_op jit(solution)/shard_map/all_to_all | solution.py:267
  123.2 0.1 broadcast_in_dim.25
  123.4 29.0 %all_to_all.23 = bf16[16,136,512]{2,1,0:T(8,128)(2,1)S(1)} all-to-all(bf16[16,136,512]{2,1,0:T(8,128)(2,1)S(1)} %broadcast_in_dim.25), channel_id=1, replica_groups=mesh['section'=2,'zh'=4,'zl'=2,'yh'=4,'yl'=2,'x'=4] {'zl','yl','x'}, dimensions={0} | all-to-all | bytes 4456448 | tf_op jit(solution)/shard_map/all_to_all | solution.py:267
  152.4 0.6 copy.16
  153.0 0.7 copy.13
  153.7 2.6 %slice.38 = f32[16,128,512]{2,1,0:T(8,128)} slice(bf16[16,136,512]{2,1,0:T(8,128)(2,1)S(1)} %all_to_all.23), slice={[0:16], [0:128], [0:512]} | slice | bytes 8388608 | tf_op jit(solution)/shard_map/slice | solution.py:300
  (17 shorter events, 0.2 us)
Async XLA Ops:
  0.6 7.8 %collective-permute-start.1 = (bf16[4,512,512]{2,1,0:T(8,128)(2,1)}, bf16[4,512,512]{2,1,0:T(8,128)(2,1)S(1)}, u32[]{:S(2)}, u32[]{:S(2)}) collective-permute-start(bf16[4,512,512]{2,1,0:T(8,128)(2,1)} %point_own.1), channel_id=1, source_target_pairs={{0,256},{256,0},{1,257},{257,1},{2,258},{258,2},{3,259},{259,3},{4... | collective-permute-start | bytes 6291464 | tf_op jit(solution)/shard_map/ppermute | solution.py:263
  5.0 3.4 %copy-start.1 = (f32[4,11,512]{2,1,0:T(8,128)}, f32[4,11,512]{2,1,0:T(8,128)S(1)}, u32[]{:S(2)}) copy-start(f32[4,11,512]{2,1,0:T(8,128)S(1)} %maximum_maximum_fusion.vec_own) | copy-start | bytes 270340
  5.0 3.4 %collective-permute-start = (f32[4,11,512]{2,1,0:T(8,128)S(1)}, f32[4,11,512]{2,1,0:T(8,128)S(1)}, u32[]{:S(2)}, u32[]{:S(2)}) collective-permute-start(f32[4,11,512]{2,1,0:T(8,128)S(1)} %maximum_maximum_fusion.vec_own), channel_id=1, source_target_pairs={{0,256},{256,0},{1,257},{257,1},{2,258},{258,2},{3,259},{259,3},{4... | collective-permute-start | bytes 270344 | tf_op jit(solution)/shard_map/ppermute | solution.py:263
  8.4 0.6 copy-start.2
  8.4 1.4 copy-start
  35.5 6.5 %collective-permute-start.2 = (bf16[16,136,512]{2,1,0:T(8,128)(2,1)}, bf16[16,136,512]{2,1,0:T(8,128)(2,1)S(1)}, u32[]{:S(2)}, u32[]{:S(2)}) collective-permute-start(bf16[16,136,512]{2,1,0:T(8,128)(2,1)} %get-tuple-element.6), channel_id=1, source_target_pairs={{0,256},{256,0},{1,257},{257,1},{2,258},{258,2},{3,259},{259,3},{4... | collective-permute-start | bytes 6684680 | tf_op jit(solution)/shard_map/ppermute | solution.py:263

commit v3 on v2

v3 whole, which is shorter than its diff:
```python
from functools import partial

import jax
import jax.numpy as jnp
from jax import lax
from jax.experimental import pallas as pl
from jax.experimental.pallas import tpu as pltpu
from jax.sharding import Mesh, PartitionSpec as P

EPSILON = 1e-06
f32, bf16 = jnp.float32, jnp.bfloat16
LANES = 128
QUARTERS = 4
NEAR = ("zl", "yl", "x")
FAR = ("zh", "yh")


def cells_kernel(
    where_, images, cotangent, vec_own, vec_far, point_own, point_far,
    kept, sent,
    point, vec, folded, packed, grads, final,
    state_a, state_b, normed_a, normed_b, inverse_a, inverse_b, slope_a, slope_b, act_a, act_b,
    grad_act_a, grad_act_b, back_a, back_b, taps_a, taps_b, sems, out_sems,
):
    half, channels = point_own.shape[0], point_own.shape[2]
    slots = 2 * half
    block = channels // QUARTERS
    groups, height, width = images.shape[0], images.shape[2], images.shape[3]
    pixels = height * width
    share = groups // 2
    span = share * pixels
    tiles = channels // LANES
    state, normed, inverse = (state_a, state_b), (normed_a, normed_b), (inverse_a, inverse_b)
    slope, act, grad_act = (slope_a, slope_b), (act_a, act_b), (grad_act_a, grad_act_b)
    back, taps = (back_a, back_b), (taps_a, taps_b)

    mine = where_[0] * half
    theirs = half - mine
    def fetch(k):
        @pl.when(k // half == where_[0])
        def _():
            pltpu.make_async_copy(point_own.at[k % half], point.at[k], sems.at[k]).start()

        @pl.when(k // half != where_[0])
        def _():
            pltpu.make_async_copy(point_far.at[k % half], point.at[k], sems.at[k]).start()

    def arrived(k):
        pltpu.make_async_copy(point_own.at[0], point.at[k], sems.at[k]).wait()

    fetch(0)
    last = pltpu.make_async_copy(cotangent.at[:, where_[0]], final, sems.at[slots])
    for k in range(1, slots):
        fetch(k)
    last.start()
    vec[pl.ds(mine, half)] = vec_own[...]
    vec[pl.ds(theirs, half)] = vec_far[...]
    count_own = jnp.max(vec_own[0, 10:11, :]).astype(jnp.int32)
    count_far = jnp.max(vec_far[0, 10:11, :]).astype(jnp.int32)
    first = jnp.where(where_[0] == 0, count_own, count_far)
    total = count_own + count_far

    def slot_of(i):
        return jnp.where(i < first, i, half + i - first)

    for k in range(slots):
        for t in range(9):
            folded[k, t:t + 1, :] = vec[k, t:t + 1, :] * vec[k, 9:10, :]
    for m in range(groups):
        rows = slice(m % share * pixels, (m % share + 1) * pixels)
        state[m // share][rows] = images[m, 0].reshape(pixels, channels).astype(f32)

    column = lax.broadcasted_iota(jnp.int32, (width, LANES), 0)
    not_first = column > 0
    not_last = column < width - 1

    def from_left(a):
        return jnp.where(not_first, pltpu.roll(a, 1, 0), 0.0)

    def from_right(a):
        return jnp.where(not_last, pltpu.roll(a, width - 1, 0), 0.0)

    def rows_of(values):
        return [values[h * width:(h + 1) * width] for h in range(height)]

    def taps_of(k, cs):
        return [jnp.broadcast_to(folded[k, t:t + 1, cs], (width, LANES)) for t in range(9)]

    def convolve(k, s):
        for m in range(share):
            rows = slice(m * pixels, (m + 1) * pixels)
            x = state[s][rows, :]
            inv = lax.rsqrt(jnp.mean(x * x, axis=-1, keepdims=True) + EPSILON)
            inv = jnp.broadcast_to(inv, (pixels, LANES))
            inverse[s][k, rows, :] = inv
            for j in range(tiles):
                cs = slice(j * LANES, (j + 1) * LANES)
                xn = x[:, cs] * inv
                normed[s][k, rows, cs] = xn
                mid = rows_of(xn)
                src = ([from_left(a) for a in mid], mid, [from_right(a) for a in mid])
                w = taps_of(k, cs)
                acts, slopes = [], []
                for h in range(height):
                    lin = None
                    for p in range(3):
                        r = h + p - 1
                        if r < 0 or r >= height:
                            continue
                        for q in range(3):
                            term = w[p * 3 + q] * src[q][r]
                            lin = term if lin is None else lin + term
                    sig = 0.5 * jnp.tanh(0.5 * lin) + 0.5
                    a = lin * sig
                    acts.append(a)
                    slopes.append(sig + a * (1.0 - sig))
                act[s][k, rows, cs] = jnp.concatenate(acts, axis=0).astype(bf16)
                slope[s][k, rows, cs] = jnp.concatenate(slopes, axis=0)

    def project(k, s):
        for n in range(0, channels, 256):
            cs = slice(n, n + 256)
            mixed = jnp.dot(act[s][k], point[k, :, cs], preferred_element_type=f32)
            state[s][:, cs] = (state[s][:, cs] + mixed).astype(bf16).astype(f32)

    convolve(0, 0)

    def forward(i, carry):
        k = slot_of(i)
        arrived(k)
        project(k, 0)
        convolve(k, 1)
        project(k, 1)
        convolve(slot_of(i + 1), 0)
        return carry

    lax.fori_loop(0, total - 1, forward, 0)
    convolve(slot_of(total - 1), 1)
    arrived(slot_of(total - 1))
    last.wait()

    def pull_back(k, s, side):
        for n in range(0, channels, 256):
            cs = slice(n, n + 256)
            grad_act[s][:, cs] = lax.dot_general(
                grads[side, s * span:(s + 1) * span, :], point[k, cs, :],
                (((1,), (1,)), ((), ())), preferred_element_type=f32,
            )

    def unconvolve(k, s, side):
        totals = [None] * share
        for j in range(tiles):
            cs = slice(j * LANES, (j + 1) * LANES)
            w = taps_of(k, cs)
            sums = [None] * 9
            for m in range(share):
                rows = slice(m * pixels, (m + 1) * pixels)
                gl = grad_act[s][rows, cs] * slope[s][k, rows, cs]
                xn = normed[s][k, rows, cs]
                xr = rows_of(xn)
                mid = rows_of(gl)
                src = ([from_right(a) for a in mid], mid, [from_left(a) for a in mid])
                us = []
                for h in range(height):
                    u = None
                    for p in range(3):
                        r = h - p + 1
                        if r < 0 or r >= height:
                            continue
                        for q in range(3):
                            t = p * 3 + q
                            term = w[t] * src[q][r]
                            u = term if u is None else u + term
                            term = xr[h] * src[q][r]
                            sums[t] = term if sums[t] is None else sums[t] + term
                    us.append(u)
                u = jnp.concatenate(us, axis=0)
                back[s][rows, cs] = u
                totals[m] = u * xn if totals[m] is None else totals[m] + u * xn
            for t in range(9):
                taps[s][t * 8:(t + 1) * 8, cs] = sums[t]
        for m in range(share):
            rows = slice(m * pixels, (m + 1) * pixels)
            there = slice(s * span + m * pixels, s * span + (m + 1) * pixels)
            mean = jnp.sum(totals[m], axis=-1, keepdims=True) * (1.0 / channels)
            mean = jnp.broadcast_to(mean, (pixels, LANES))
            inv = inverse[s][k, rows, :]
            for j in range(tiles):
                cs = slice(j * LANES, (j + 1) * LANES)
                gx = inv * (back[s][rows, cs] - normed[s][k, rows, cs] * mean)
                gx = grads[side, there, cs].astype(f32) + gx
                grads[1 - side, there, cs] = gx.astype(bf16)

    def weigh(k, side):
        both = jnp.concatenate([act[0][k], act[1][k]], axis=0)
        g = grads[side]
        for r in range(QUARTERS):
            packed[QUARTERS * k + r, :block, :] = lax.dot_general(
                both[:, r * block:(r + 1) * block], g, (((0,), (0,)), ((), ())), preferred_element_type=f32
            ).astype(bf16)

    def summarise(k):
        gain = vec[k, 9:10, :]
        grad_gain = jnp.zeros((1, channels), f32)
        parts = []
        for t in range(9):
            both = taps[0][t * 8:(t + 1) * 8, :] + taps[1][t * 8:(t + 1) * 8, :]
            summed = jnp.sum(both, axis=0, keepdims=True)
            parts.append(summed * gain)
            grad_gain = grad_gain + vec[k, t:t + 1, :] * summed
        parts.append(grad_gain)
        for r in range(QUARTERS):
            some = parts[r * 3:r * 3 + 3]
            some = some + [jnp.zeros((8 - len(some), channels), f32)]
            packed[QUARTERS * k + r, block:block + 8, :] = jnp.concatenate(some, axis=0).astype(bf16)

    def send_out(k):
        cell = lax.rem(k, half)
        inside = packed.at[pl.ds(QUARTERS * k, QUARTERS)]
        outside = pl.ds(QUARTERS * cell, QUARTERS)

        @pl.when(lax.div(k, half) == where_[0])
        def _():
            pltpu.make_async_copy(inside, kept.at[outside], out_sems.at[k]).start()

        @pl.when(lax.div(k, half) != where_[0])
        def _():
            pltpu.make_async_copy(inside, sent.at[outside], out_sems.at[k]).start()

    for m in range(groups):
        grads[0, m * pixels:(m + 1) * pixels, :] = final[m].reshape(pixels, channels)
    pull_back(slot_of(total - 1), 0, 0)

    def backward(n, carry):
        i = total - 1 - n
        k = slot_of(i)
        side = lax.rem(n, 2)
        pull_back(k, 1, side)
        unconvolve(k, 0, side)
        weigh(k, side)
        pull_back(slot_of(jnp.maximum(i - 1, 0)), 0, 1 - side)
        unconvolve(k, 1, side)
        summarise(k)
        send_out(k)
        return carry

    lax.fori_loop(0, total, backward, 0)

    def idle(k, carry):
        @pl.when(lax.rem(k, half) >= jnp.where(k < half, first, total - first))
        def _():
            arrived(k)
            packed[pl.ds(QUARTERS * k, QUARTERS)] = jnp.zeros((QUARTERS, block + 8, channels), bf16)
            send_out(k)
        return carry

    lax.fori_loop(0, slots, idle, 0)
    for k in range(slots):
        pltpu.make_async_copy(
            packed.at[QUARTERS * k:QUARTERS * (k + 1)], kept.at[0:QUARTERS], out_sems.at[k]
        ).wait()


def run_cells(section, images, cotangent, vec_own, vec_far, point_own, point_far):
    half = point_own.shape[0]
    slots = 2 * half
    groups, unused, height, width, channels = images.shape
    total = groups * height * width
    span = total // 2
    share = (groups, 1, height, width, channels)
    out = jax.ShapeDtypeStruct((QUARTERS * half, channels // QUARTERS + 8, channels), bf16)

    def pair(shape, dtype):
        return [pltpu.VMEM(shape, dtype)] * 2

    spec = pltpu.PrefetchScalarGridSpec(
        num_scalar_prefetch=1,
        grid=(1,),
        in_specs=[
            pl.BlockSpec(share, lambda i, s: (0, s[0], 0, 0, 0)),
            pl.BlockSpec(memory_space=pl.ANY),
            pl.BlockSpec(vec_own.shape, lambda i, s: (0, 0, 0)),
            pl.BlockSpec(vec_far.shape, lambda i, s: (0, 0, 0)),
            pl.BlockSpec(memory_space=pl.ANY),
            pl.BlockSpec(memory_space=pl.ANY),
        ],
        out_specs=[pl.BlockSpec(memory_space=pl.ANY)] * 2,
        scratch_shapes=[
            pltpu.VMEM((slots, channels, channels), bf16),
            pltpu.VMEM((slots, 11, channels), f32),
            pltpu.VMEM((slots, 9, channels), f32),
            pltpu.VMEM((QUARTERS * slots, channels // QUARTERS + 8, channels), bf16),
            pltpu.VMEM((2, total, channels), bf16),
            pltpu.VMEM((groups, height, width, channels), bf16),
            *pair((span, channels), f32),
            *pair((slots, span, channels), f32),
            *pair((slots, span, LANES), f32),
            *pair((slots, span, channels), f32),
            *pair((slots, span, channels), bf16),
            *pair((span, channels), f32),
            *pair((span, channels), f32),
            *pair((72, channels), f32),
            pltpu.SemaphoreType.DMA((slots + 1,)),
            pltpu.SemaphoreType.DMA((slots,)),
        ],
    )
    return pl.pallas_call(
        cells_kernel,
        grid_spec=spec,
        out_shape=[out, out],
        compiler_params=pltpu.CompilerParams(vmem_limit_bytes=56 << 20),
        name="cells",
    )(section, images, cotangent, vec_own, vec_far, point_own, point_far)


def swapped(block):
    return lax.ppermute(block, "section", [(0, 1), (1, 0)])


def exchanged(block, axes):
    return lax.all_to_all(block, axes, 0, 0, tiled=True)


def added(blocks):
    return jnp.sum(blocks.astype(f32), axis=0)


def local(images, cotangent, counts, gains, depthwise, pointwise):
    cells, channels = gains.shape
    section = lax.axis_index("section").astype(jnp.int32)
    point_far = swapped(pointwise)
    vec_own = jnp.concatenate(
        [depthwise, gains[:, None, :], jnp.broadcast_to(counts.astype(f32)[:, None, None], (cells, 1, channels))],
        axis=1,
    )
    vec_far = swapped(vec_own)
    kept, sent = run_cells(section[None], images, cotangent, vec_own, vec_far, pointwise, point_far)
    summed = (kept.astype(f32) + swapped(sent).astype(f32)).astype(bf16)

    near, rows, unused = summed.shape
    rows -= 8
    far = lax.axis_size(FAR)
    part = added(exchanged(summed, NEAR))
    strip = part[rows:rows + 4].reshape(-1, LANES)
    strip = jnp.pad(strip, ((0, rows - strip.shape[0]), (0, 0)))
    wide = jnp.concatenate([part[:rows], strip], axis=1).astype(bf16).reshape(far, rows // far, channels + LANES)
    piece = added(exchanged(wide, FAR)).astype(bf16)

    back = exchanged(jnp.broadcast_to(piece, wide.shape), FAR).reshape(rows, channels + LANES)
    small = back[:32, channels:].reshape(8, channels)
    back = jnp.concatenate([back[:, :channels], small], axis=0)
    out = exchanged(jnp.broadcast_to(back, summed.shape), NEAR).astype(f32)
    small = out[:, rows:rows + 3].reshape(cells, 3 * QUARTERS, channels)
    return out[:, :rows].reshape(cells, channels, channels), small[:, :9], small[:, 9]


def solution(mesh):
    grid = Mesh(mesh.devices.reshape(2, 4, 2, 4, 2, 4), ("section", "zh", "zl", "yh", "yl", "x"))
    data = ("zh", "zl", "yh", "yl", "x")
    placed = (
        P(None, data, None, None, None),
        P(None, data, None, None, None),
        P("section"),
        P("section", None),
        P("section", None, None),
        P("section", None, None),
    )
    return jax.shard_map(
        local,
        mesh=grid,
        in_specs=placed,
        out_specs=(P("section", None, None), P("section", None, None), P("section", None)),
        check_vma=False,
    )
```

time: 157 us -> 146 us (0.930)
  Pallas kernels: 25.8 us -> 15.2 us
    pallas_call x1, Pallas kernels: 25.8 us -> 15.2 us  [run_cells(): pl.pallas_call(cells_kernel, grid_spec=spec, out_shape=[out, out], compil...]
where the time goes in v3:
time: 146 us
  blocking collectives  107 us (73%)
  Pallas kernels  15.2 us (10%)
  local copies, waits for them, and re-layouts  7.24 us (5%)
  starting transfers between devices  6.6 us (5%)
  waiting for transfers between devices  5.13 us (4%)
  other arithmetic  2.73 us (2%)
    all_to_all x4, blocking collectives, exchanged(): return lax.all_to_all(block, axes, 0, 0, tiled=True)  107 us
    pallas_call x1, Pallas kernels, run_cells(): pl.pallas_call(cells_kernel, grid_spec=spec, out_shape=[out, out], compil...  15.2 us
    ppermute x3, starting transfers between devices, swapped(): return lax.ppermute(block, 'section', [(0, 1), (1, 0)])  6.6 us
    ppermute x3, waiting for transfers between devices, swapped(): return lax.ppermute(block, 'section', [(0, 1), (1, 0)])  5.13 us
    unnamed x9, local copies, waits for them, and re-layouts  3.54 us
  transfers between devices with their start and end apart: 3, of which 2 were waited for; matrix products, arithmetic and copies ran while one was open for 1% of the time, Pallas kernels for 0%

profile of v3, /device:TPU:2, one launch (start us, length us, event | category | flops | bytes accessed | tf_op | source)
XLA Modules:
  0.0 145.7 jit_solution(10326681843288038860)
XLA Ops:
  0.6 1.9 %collective-permute-start.1 = (bf16[4,512,512]{2,1,0:T(8,128)(2,1)}, bf16[4,512,512]{2,1,0:T(8,128)(2,1)S(1)}, u32[]{:S(2)}, u32[]{:S(2)}) collective-permute-start(bf16[4,512,512]{2,1,0:T(8,128)(2,1)} %point_own.1), channel_id=1, source_target_pairs={{0,256},{256,0},{1,257},{257,1},{2,258},{258,2},{3,259},{259,3},{4... | collective-permute-start | bytes 6291464 | tf_op jit(solution)/shard_map/ppermute | solution.py:317
  3.2 0.7 broadcast_in_dim.21
  3.9 0.9 copy.12
  4.8 0.1 pad.12.clone
  4.9 0.1 maximum_maximum_fusion.vec_own
  5.0 0.0 copy-start.1
  5.0 2.4 %collective-permute-start = (f32[4,11,512]{2,1,0:T(8,128)S(1)}, f32[4,11,512]{2,1,0:T(8,128)S(1)}, u32[]{:S(2)}, u32[]{:S(2)}) collective-permute-start(f32[4,11,512]{2,1,0:T(8,128)S(1)} %maximum_maximum_fusion.vec_own), channel_id=1, source_target_pairs={{0,256},{256,0},{1,257},{257,1},{2,258},{258,2},{3,259},{259,3},{4... | collective-permute-start | bytes 270344 | tf_op jit(solution)/shard_map/ppermute | solution.py:317
  7.4 1.0 collective-permute-done.vec_far
  8.4 0.0 collective-permute-done.1.point_far
  8.4 0.6 copy-done.2
  9.0 0.7 copy-done
  9.7 15.2 %cells.1 = (bf16[16,136,512]{2,1,0:T(8,128)(2,1)}, bf16[16,136,512]{2,1,0:T(8,128)(2,1)}) custom-call(s32[1]{0:T(128)} %bitcast.where_, bf16[4,2,8,8,512]{4,3,2,1,0:T(8,128)(2,1)} %images.1, bf16[4,2,8,8,512]{4,3,2,1,0:T(8,128)(2,1)} %cotangent.1, f32[4,11,512]{2,1,0:T(8,128)} %copy-done.1, f32[4,11,512]{2,1,0:T(8,128)} %copy-done.2, ...), custom_call_target="tpu_custom_call" | custom-call | tf_op jit(solution)/shard_map/cells/pallas_call | solution.py:307
  24.9 2.3 %collective-permute-start.2 = (bf16[16,136,512]{2,1,0:T(8,128)(2,1)}, bf16[16,136,512]{2,1,0:T(8,128)(2,1)S(1)}, u32[]{:S(2)}, u32[]{:S(2)}) collective-permute-start(bf16[16,136,512]{2,1,0:T(8,128)(2,1)} %get-tuple-element.6), channel_id=1, source_target_pairs={{0,256},{256,0},{1,257},{257,1},{2,258},{258,2},{3,259},{259,3},{4... | collective-permute-start | bytes 6684680 | tf_op jit(solution)/shard_map/ppermute | solution.py:317
  27.2 4.2 %collective-permute-done.2 = bf16[16,136,512]{2,1,0:T(8,128)(2,1)S(1)} collective-permute-done((bf16[16,136,512]{2,1,0:T(8,128)(2,1)}, bf16[16,136,512]{2,1,0:T(8,128)(2,1)S(1)}, u32[]{:S(2)}, u32[]{:S(2)}) %collective-permute-start.2) | collective-permute-done | bytes 2228256 | tf_op jit(solution)/shard_map/ppermute | solution.py:317
  31.4 2.3 %add_convert_fusion = bf16[16,136,512]{2,1,0:T(8,128)(2,1)S(1)} fusion(bf16[16,136,512]{2,1,0:T(8,128)(2,1)S(1)} %collective-permute-done.2, bf16[16,136,512]{2,1,0:T(8,128)(2,1)} %get-tuple-element.5), kind=kLoop, calls=%fused_computation | loop fusion | flops 4456448 | bytes 6684672 | tf_op jit(solution)/shard_map/convert_element_type | solution.py:338
  33.7 37.3 %all_to_all.20 = bf16[16,136,512]{2,1,0:T(8,128)(2,1)S(1)} all-to-all(bf16[16,136,512]{2,1,0:T(8,128)(2,1)S(1)} %add_convert_fusion), channel_id=1, replica_groups=mesh['section'=2,'zh'=4,'zl'=2,'yh'=4,'yl'=2,'x'=4] {'zl','yl','x'}, dimensions={0} | all-to-all | bytes 4456448 | tf_op jit(solution)/shard_map/all_to_all | solution.py:321
  71.0 0.3 reduce.1
  71.4 25.0 %all_to_all.21 = bf16[16,8,640]{2,1,0:T(8,128)(2,1)S(1)} all-to-all(bf16[16,8,640]{2,1,0:T(8,128)(2,1)S(1)} %pad_maximum_fusion), channel_id=1, replica_groups=mesh['section'=2,'zh'=4,'zl'=2,'yh'=4,'yl'=2,'x'=4] {'zh','yh'}, dimensions={0} | all-to-all | bytes 327680 | tf_op jit(solution)/shard_map/all_to_all | solution.py:321
  96.4 16.1 %all_to_all.22 = bf16[16,8,640]{2,1,0:T(8,128)(2,1)S(1)} all-to-all(bf16[16,8,640]{2,1,0:T(8,128)(2,1)S(1)} %broadcast_in_dim.24), channel_id=1, replica_groups=mesh['section'=2,'zh'=4,'zl'=2,'yh'=4,'yl'=2,'x'=4] {'zh','yh'}, dimensions={0} | all-to-all | bytes 327680 | tf_op jit(solution)/shard_map/all_to_all | solution.py:321
  112.6 0.1 broadcast_in_dim.25
  112.8 29.0 %all_to_all.23 = bf16[16,136,512]{2,1,0:T(8,128)(2,1)S(1)} all-to-all(bf16[16,136,512]{2,1,0:T(8,128)(2,1)S(1)} %broadcast_in_dim.25), channel_id=1, replica_groups=mesh['section'=2,'zh'=4,'zl'=2,'yh'=4,'yl'=2,'x'=4] {'zl','yl','x'}, dimensions={0} | all-to-all | bytes 4456448 | tf_op jit(solution)/shard_map/all_to_all | solution.py:321
  141.8 0.6 copy.16
  142.4 0.7 copy.13
  143.1 2.6 %slice.38 = f32[16,128,512]{2,1,0:T(8,128)} slice(bf16[16,136,512]{2,1,0:T(8,128)(2,1)S(1)} %all_to_all.23), slice={[0:16], [0:128], [0:512]} | slice | bytes 8388608 | tf_op jit(solution)/shard_map/slice | solution.py:354
  (17 shorter events, 0.2 us)
Async XLA Ops:
  0.6 7.8 %collective-permute-start.1 = (bf16[4,512,512]{2,1,0:T(8,128)(2,1)}, bf16[4,512,512]{2,1,0:T(8,128)(2,1)S(1)}, u32[]{:S(2)}, u32[]{:S(2)}) collective-permute-start(bf16[4,512,512]{2,1,0:T(8,128)(2,1)} %point_own.1), channel_id=1, source_target_pairs={{0,256},{256,0},{1,257},{257,1},{2,258},{258,2},{3,259},{259,3},{4... | collective-permute-start | bytes 6291464 | tf_op jit(solution)/shard_map/ppermute | solution.py:317
  5.0 3.4 %copy-start.1 = (f32[4,11,512]{2,1,0:T(8,128)}, f32[4,11,512]{2,1,0:T(8,128)S(1)}, u32[]{:S(2)}) copy-start(f32[4,11,512]{2,1,0:T(8,128)S(1)} %maximum_maximum_fusion.vec_own) | copy-start | bytes 270340
  5.0 3.4 %collective-permute-start = (f32[4,11,512]{2,1,0:T(8,128)S(1)}, f32[4,11,512]{2,1,0:T(8,128)S(1)}, u32[]{:S(2)}, u32[]{:S(2)}) collective-permute-start(f32[4,11,512]{2,1,0:T(8,128)S(1)} %maximum_maximum_fusion.vec_own), channel_id=1, source_target_pairs={{0,256},{256,0},{1,257},{257,1},{2,258},{258,2},{3,259},{259,3},{4... | collective-permute-start | bytes 270344 | tf_op jit(solution)/shard_map/ppermute | solution.py:317
  8.4 0.6 copy-start.2
  8.4 1.4 copy-start
  24.9 6.5 %collective-permute-start.2 = (bf16[16,136,512]{2,1,0:T(8,128)(2,1)}, bf16[16,136,512]{2,1,0:T(8,128)(2,1)S(1)}, u32[]{:S(2)}, u32[]{:S(2)}) collective-permute-start(bf16[16,136,512]{2,1,0:T(8,128)(2,1)} %get-tuple-element.6), channel_id=1, source_target_pairs={{0,256},{256,0},{1,257},{257,1},{2,258},{258,2},{3,259},{259,3},{4... | collective-permute-start | bytes 6684680 | tf_op jit(solution)/shard_map/ppermute | solution.py:317

commit v4 on v3

--- a/solution.py
+++ b/solution.py
@@ -18,7 +18,7 @@
 def cells_kernel(
     where_, images, cotangent, vec_own, vec_far, point_own, point_far,
     kept, sent,
-    point, vec, folded, packed, grads, final,
+    point, vec, folded, packed, grads, opening, final,
     state_a, state_b, normed_a, normed_b, inverse_a, inverse_b, slope_a, slope_b, act_a, act_b,
     grad_act_a, grad_act_b, back_a, back_b, taps_a, taps_b, sems, out_sems,
 ):
@@ -48,15 +48,18 @@
     def arrived(k):
         pltpu.make_async_copy(point_own.at[0], point.at[k], sems.at[k]).wait()
 
+    start = pltpu.make_async_copy(images.at[:, where_[0]], opening, sems.at[slots + 1])
+    start.start()
     fetch(0)
     last = pltpu.make_async_copy(cotangent.at[:, where_[0]], final, sems.at[slots])
     for k in range(1, slots):
         fetch(k)
     last.start()
-    vec[pl.ds(mine, half)] = vec_own[...]
-    vec[pl.ds(theirs, half)] = vec_far[...]
-    count_own = jnp.max(vec_own[0, 10:11, :]).astype(jnp.int32)
-    count_far = jnp.max(vec_far[0, 10:11, :]).astype(jnp.int32)
+    for c in range(half):
+        vec[mine + c] = vec_own[:, c, :]
+        vec[theirs + c] = vec_far[:, c, :]
+    count_own = jnp.max(vec_own[10, 0:1, :]).astype(jnp.int32)
+    count_far = jnp.max(vec_far[10, 0:1, :]).astype(jnp.int32)
     first = jnp.where(where_[0] == 0, count_own, count_far)
     total = count_own + count_far
 
@@ -66,9 +69,10 @@
     for k in range(slots):
         for t in range(9):
             folded[k, t:t + 1, :] = vec[k, t:t + 1, :] * vec[k, 9:10, :]
+    start.wait()
     for m in range(groups):
         rows = slice(m % share * pixels, (m % share + 1) * pixels)
-        state[m // share][rows] = images[m, 0].reshape(pixels, channels).astype(f32)
+        state[m // share][rows] = opening[m].reshape(pixels, channels).astype(f32)
 
     column = lax.broadcasted_iota(jnp.int32, (width, LANES), 0)
     not_first = column > 0
@@ -147,7 +151,7 @@
                 (((1,), (1,)), ((), ())), preferred_element_type=f32,
             )
 
-    def unconvolve(k, s, side):
+    def unconvolve(k, s, side, onward=True):
         totals = [None] * share
         for j in range(tiles):
             cs = slice(j * LANES, (j + 1) * LANES)
@@ -169,17 +173,20 @@
                             continue
                         for q in range(3):
                             t = p * 3 + q
-                            term = w[t] * src[q][r]
-                            u = term if u is None else u + term
+                            if onward:
+                                term = w[t] * src[q][r]
+                                u = term if u is None else u + term
                             term = xr[h] * src[q][r]
                             sums[t] = term if sums[t] is None else sums[t] + term
                     us.append(u)
+                if not onward:
+                    continue
                 u = jnp.concatenate(us, axis=0)
                 back[s][rows, cs] = u
                 totals[m] = u * xn if totals[m] is None else totals[m] + u * xn
             for t in range(9):
                 taps[s][t * 8:(t + 1) * 8, cs] = sums[t]
-        for m in range(share):
+        for m in range(share if onward else 0):
             rows = slice(m * pixels, (m + 1) * pixels)
             there = slice(s * span + m * pixels, s * span + (m + 1) * pixels)
             mean = jnp.sum(totals[m], axis=-1, keepdims=True) * (1.0 / channels)
@@ -238,13 +245,20 @@
         pull_back(k, 1, side)
         unconvolve(k, 0, side)
         weigh(k, side)
-        pull_back(slot_of(jnp.maximum(i - 1, 0)), 0, 1 - side)
+        pull_back(slot_of(i - 1), 0, 1 - side)
         unconvolve(k, 1, side)
         summarise(k)
         send_out(k)
         return carry
 
-    lax.fori_loop(0, total, backward, 0)
+    lax.fori_loop(0, total - 1, backward, 0)
+    side = lax.rem(total - 1, 2)
+    pull_back(0, 1, side)
+    unconvolve(0, 0, side, False)
+    weigh(0, side)
+    unconvolve(0, 1, side, False)
+    summarise(0)
+    send_out(0)
 
     def idle(k, carry):
         @pl.when(lax.rem(k, half) >= jnp.where(k < half, first, total - first))
@@ -267,7 +281,6 @@
     groups, unused, height, width, channels = images.shape
     total = groups * height * width
     span = total // 2
-    share = (groups, 1, height, width, channels)
     out = jax.ShapeDtypeStruct((QUARTERS * half, channels // QUARTERS + 8, channels), bf16)
 
     def pair(shape, dtype):
@@ -277,11 +290,11 @@
         num_scalar_prefetch=1,
         grid=(1,),
         in_specs=[
-            pl.BlockSpec(share, lambda i, s: (0, s[0], 0, 0, 0)),
-            pl.BlockSpec(memory_space=pl.ANY),
+            pl.BlockSpec(memory_space=pltpu.HBM),
+            pl.BlockSpec(memory_space=pltpu.HBM),
             pl.BlockSpec(vec_own.shape, lambda i, s: (0, 0, 0)),
             pl.BlockSpec(vec_far.shape, lambda i, s: (0, 0, 0)),
-            pl.BlockSpec(memory_space=pl.ANY),
+            pl.BlockSpec(memory_space=pltpu.HBM),
             pl.BlockSpec(memory_space=pl.ANY),
         ],
         out_specs=[pl.BlockSpec(memory_space=pl.ANY)] * 2,
@@ -292,6 +305,7 @@
             pltpu.VMEM((QUARTERS * slots, channels // QUARTERS + 8, channels), bf16),
             pltpu.VMEM((2, total, channels), bf16),
             pltpu.VMEM((groups, height, width, channels), bf16),
+            pltpu.VMEM((groups, height, width, channels), bf16),
             *pair((span, channels), f32),
             *pair((slots, span, channels), f32),
             *pair((slots, span, LANES), f32),
@@ -300,7 +314,7 @@
             *pair((span, channels), f32),
             *pair((span, channels), f32),
             *pair((72, channels), f32),
-            pltpu.SemaphoreType.DMA((slots + 1,)),
+            pltpu.SemaphoreType.DMA((slots + 2,)),
             pltpu.SemaphoreType.DMA((slots,)),
         ],
     )
@@ -308,7 +322,7 @@
         cells_kernel,
         grid_spec=spec,
         out_shape=[out, out],
-        compiler_params=pltpu.CompilerParams(vmem_limit_bytes=56 << 20),
+        compiler_params=pltpu.CompilerParams(vmem_limit_bytes=26 << 20),
         name="cells",
     )(section, images, cotangent, vec_own, vec_far, point_own, point_far)
 
@@ -330,10 +344,17 @@
     section = lax.axis_index("section").astype(jnp.int32)
     point_far = swapped(pointwise)
     vec_own = jnp.concatenate(
-        [depthwise, gains[:, None, :], jnp.broadcast_to(counts.astype(f32)[:, None, None], (cells, 1, channels))],
-        axis=1,
+        [
+            jnp.transpose(depthwise, (1, 0, 2)),
+            gains[None],
+            jnp.broadcast_to(counts.astype(f32)[:, None, None], (1, cells, channels)),
+        ],
+        axis=0,
     )
     vec_far = swapped(vec_own)
+    images, cotangent, pointwise = (
+        pltpu.with_memory_space_constraint(a, pltpu.HBM) for a in (images, cotangent, pointwise)
+    )
     kept, sent = run_cells(section[None], images, cotangent, vec_own, vec_far, pointwise, point_far)
     summed = (kept.astype(f32) + swapped(sent).astype(f32)).astype(bf16)
 

time: 146 us -> 141 us (0.966)
  local copies, waits for them, and re-layouts: 7.24 us -> 4.27 us
    unnamed x9 -> x2, local copies, waits for them, and re-layouts: 3.54 us -> 1.28 us
    convert_element_type x1, other arithmetic: 2.25 us -> 0.72 us  [local(): summed = (kept.astype(f32) + swapped(sent).astype(f32)).astype(bf16)]
where the time goes in v4:
time: 141 us
  blocking collectives  107 us (76%)
  Pallas kernels  14 us (10%)
  starting transfers between devices  6.6 us (5%)
  waiting for transfers between devices  4.88 us (3%)
  local copies, waits for them, and re-layouts  4.27 us (3%)
  other arithmetic  2.1 us (1%)
    all_to_all x4, blocking collectives, exchanged(): return lax.all_to_all(block, axes, 0, 0, tiled=True)  107 us
    pallas_call x1, Pallas kernels, run_cells(): pl.pallas_call(cells_kernel, grid_spec=spec, out_shape=[out, out], compil...  14 us
    ppermute x3, starting transfers between devices, swapped(): return lax.ppermute(block, 'section', [(0, 1), (1, 0)])  6.6 us
    ppermute x3, waiting for transfers between devices, swapped(): return lax.ppermute(block, 'section', [(0, 1), (1, 0)])  4.88 us
  transfers between devices with their start and end apart: 3, of which 2 were waited for; matrix products, arithmetic and copies ran while one was open for 1% of the time, Pallas kernels for 0%

profile of v4, /device:TPU:2, one launch (start us, length us, event | category | flops | bytes accessed | tf_op | source)
XLA Modules:
  0.0 140.5 jit_solution(9450608550161274103)
XLA Ops:
  0.6 1.9 %collective-permute-start.1 = (bf16[4,512,512]{2,1,0:T(8,128)(2,1)}, bf16[4,512,512]{2,1,0:T(8,128)(2,1)S(1)}, u32[]{:S(2)}, u32[]{:S(2)}) collective-permute-start(bf16[4,512,512]{2,1,0:T(8,128)(2,1)} %point_own.1), channel_id=1, source_target_pairs={{0,256},{256,0},{1,257},{257,1},{2,258},{258,2},{3,259},{259,3},{4... | collective-permute-start | bytes 6291464 | tf_op jit(solution)/shard_map/ppermute | solution.py:331
  3.2 0.1 pad.12.clone
  3.3 1.0 maximum_maximum_fusion.vec_own
  4.3 2.4 %collective-permute-start = (f32[11,4,512]{2,1,0:T(4,128)S(1)}, f32[11,4,512]{2,1,0:T(4,128)S(1)}, u32[]{:S(2)}, u32[]{:S(2)}) collective-permute-start(f32[11,4,512]{2,1,0:T(4,128)S(1)} %maximum_maximum_fusion.vec_own), channel_id=1, source_target_pairs={{0,256},{256,0},{1,257},{257,1},{2,258},{258,2},{3,259},{259,3},{4... | collective-permute-start | bytes 270344 | tf_op jit(solution)/shard_map/ppermute | solution.py:331
  6.7 0.9 collective-permute-done.vec_far
  7.6 0.0 collective-permute-done.1.point_far
  7.6 14.0 %cells.1 = (bf16[16,136,512]{2,1,0:T(8,128)(2,1)S(1)}, bf16[16,136,512]{2,1,0:T(8,128)(2,1)S(1)}) custom-call(s32[1]{0:T(128)} %bitcast.where_, bf16[4,2,8,8,512]{4,3,2,1,0:T(8,128)(2,1)} %images.1, bf16[4,2,8,8,512]{4,3,2,1,0:T(8,128)(2,1)} %cotangent.1, f32[11,4,512]{2,1,0:T(4,128)S(1)} %maximum_maximum_fusion.vec_own, ...), custom_call_target="tpu_custom_call" | custom-call | tf_op jit(solution)/shard_map/cells/pallas_call | solution.py:321
  21.6 2.3 %collective-permute-start.2 = (bf16[16,136,512]{2,1,0:T(8,128)(2,1)S(1)}, bf16[16,136,512]{2,1,0:T(8,128)(2,1)S(1)}, u32[]{:S(2)}, u32[]{:S(2)}) collective-permute-start(bf16[16,136,512]{2,1,0:T(8,128)(2,1)S(1)} %get-tuple-element.6), channel_id=1, source_target_pairs={{0,256},{256,0},{1,257},{257,1},{2,258},{258,2},{3,259},{259,3},{4... | collective-permute-start | bytes 6684680 | tf_op jit(solution)/shard_map/ppermute | solution.py:331
  23.8 4.0 %collective-permute-done.2 = bf16[16,136,512]{2,1,0:T(8,128)(2,1)S(1)} collective-permute-done((bf16[16,136,512]{2,1,0:T(8,128)(2,1)S(1)}, bf16[16,136,512]{2,1,0:T(8,128)(2,1)S(1)}, u32[]{:S(2)}, u32[]{:S(2)}) %collective-permute-start.2) | collective-permute-done | bytes 2228256 | tf_op jit(solution)/shard_map/ppermute | solution.py:331
  27.8 0.7 add_convert_fusion
  28.5 37.3 %all_to_all.20 = bf16[16,136,512]{2,1,0:T(8,128)(2,1)S(1)} all-to-all(bf16[16,136,512]{2,1,0:T(8,128)(2,1)S(1)} %add_convert_fusion), channel_id=1, replica_groups=mesh['section'=2,'zh'=4,'zl'=2,'yh'=4,'yl'=2,'x'=4] {'zl','yl','x'}, dimensions={0} | all-to-all | bytes 4456448 | tf_op jit(solution)/shard_map/all_to_all | solution.py:335
  65.8 0.3 reduce.1
  66.2 25.0 %all_to_all.21 = bf16[16,8,640]{2,1,0:T(8,128)(2,1)S(1)} all-to-all(bf16[16,8,640]{2,1,0:T(8,128)(2,1)S(1)} %pad_maximum_fusion), channel_id=1, replica_groups=mesh['section'=2,'zh'=4,'zl'=2,'yh'=4,'yl'=2,'x'=4] {'zh','yh'}, dimensions={0} | all-to-all | bytes 327680 | tf_op jit(solution)/shard_map/all_to_all | solution.py:335
  91.3 16.1 %all_to_all.22 = bf16[16,8,640]{2,1,0:T(8,128)(2,1)S(1)} all-to-all(bf16[16,8,640]{2,1,0:T(8,128)(2,1)S(1)} %broadcast_in_dim.24), channel_id=1, replica_groups=mesh['section'=2,'zh'=4,'zl'=2,'yh'=4,'yl'=2,'x'=4] {'zh','yh'}, dimensions={0} | all-to-all | bytes 327680 | tf_op jit(solution)/shard_map/all_to_all | solution.py:335
  107.5 0.1 broadcast_in_dim.25
  107.6 28.9 %all_to_all.23 = bf16[16,136,512]{2,1,0:T(8,128)(2,1)S(1)} all-to-all(bf16[16,136,512]{2,1,0:T(8,128)(2,1)S(1)} %broadcast_in_dim.25), channel_id=1, replica_groups=mesh['section'=2,'zh'=4,'zl'=2,'yh'=4,'yl'=2,'x'=4] {'zl','yl','x'}, dimensions={0} | all-to-all | bytes 4456448 | tf_op jit(solution)/shard_map/all_to_all | solution.py:335
  136.7 0.6 copy.13
  137.3 0.7 copy.10
  137.9 2.6 %slice.38 = f32[16,128,512]{2,1,0:T(8,128)} slice(bf16[16,136,512]{2,1,0:T(8,128)(2,1)S(1)} %all_to_all.23), slice={[0:16], [0:128], [0:512]} | slice | bytes 8388608 | tf_op jit(solution)/shard_map/slice | solution.py:375
  (14 shorter events, 0.2 us)
Async XLA Ops:
  0.6 7.0 %collective-permute-start.1 = (bf16[4,512,512]{2,1,0:T(8,128)(2,1)}, bf16[4,512,512]{2,1,0:T(8,128)(2,1)S(1)}, u32[]{:S(2)}, u32[]{:S(2)}) collective-permute-start(bf16[4,512,512]{2,1,0:T(8,128)(2,1)} %point_own.1), channel_id=1, source_target_pairs={{0,256},{256,0},{1,257},{257,1},{2,258},{258,2},{3,259},{259,3},{4... | collective-permute-start | bytes 6291464 | tf_op jit(solution)/shard_map/ppermute | solution.py:331
  4.3 3.3 %collective-permute-start = (f32[11,4,512]{2,1,0:T(4,128)S(1)}, f32[11,4,512]{2,1,0:T(4,128)S(1)}, u32[]{:S(2)}, u32[]{:S(2)}) collective-permute-start(f32[11,4,512]{2,1,0:T(4,128)S(1)} %maximum_maximum_fusion.vec_own), channel_id=1, source_target_pairs={{0,256},{256,0},{1,257},{257,1},{2,258},{258,2},{3,259},{259,3},{4... | collective-permute-start | bytes 270344 | tf_op jit(solution)/shard_map/ppermute | solution.py:331
  21.6 6.2 %collective-permute-start.2 = (bf16[16,136,512]{2,1,0:T(8,128)(2,1)S(1)}, bf16[16,136,512]{2,1,0:T(8,128)(2,1)S(1)}, u32[]{:S(2)}, u32[]{:S(2)}) collective-permute-start(bf16[16,136,512]{2,1,0:T(8,128)(2,1)S(1)} %get-tuple-element.6), channel_id=1, source_target_pairs={{0,256},{256,0},{1,257},{257,1},{2,258},{258,2},{3,259},{259,3},{4... | collective-permute-start | bytes 6684680 | tf_op jit(solution)/shard_map/ppermute | solution.py:331

commit v5 on v4

--- a/solution.py
+++ b/solution.py
@@ -327,6 +327,44 @@
     )(section, images, cotangent, vec_own, vec_far, point_own, point_far)
 
 
+def widen_kernel(totals, grad_point, grad_depth, grad_gain, wide, sems):
+    count, rows = wide.shape[0], wide.shape[1]
+    copies = []
+    for n in range(count):
+        wide[n] = totals[n, :rows, :].astype(f32)
+        where = grad_point.at[n // QUARTERS, pl.ds(n % QUARTERS * rows, rows)]
+        copies.append(pltpu.make_async_copy(wide.at[n], where, sems.at[n]))
+        copies[n].start()
+    for n in range(count):
+        cell, r = n // QUARTERS, n % QUARTERS
+        some = totals[n, rows:rows + 8, :].astype(f32)
+        for i in range(3):
+            t = 3 * r + i
+            if t < 9:
+                grad_depth[t, cell:cell + 1, :] = some[i:i + 1]
+            elif t == 9:
+                grad_gain[cell:cell + 1, :] = some[i:i + 1]
+    for copy in copies:
+        copy.wait()
+
+
+def widened(totals, cells, channels):
+    count, rows = totals.shape[0], totals.shape[1] - 8
+    return pl.pallas_call(
+        widen_kernel,
+        in_specs=[pl.BlockSpec(memory_space=pltpu.VMEM)],
+        out_specs=[pl.BlockSpec(memory_space=pl.ANY)] + [pl.BlockSpec(memory_space=pltpu.VMEM)] * 2,
+        out_shape=[
+            jax.ShapeDtypeStruct((cells, channels, channels), f32),
+            jax.ShapeDtypeStruct((9, cells, channels), f32),
+            jax.ShapeDtypeStruct((cells, channels), f32),
+        ],
+        scratch_shapes=[pltpu.VMEM((count, rows, channels), f32), pltpu.SemaphoreType.DMA((count,))],
+        compiler_params=pltpu.CompilerParams(vmem_limit_bytes=12 << 20),
+        name="widen",
+    )(totals)
+
+
 def swapped(block):
     return lax.ppermute(block, "section", [(0, 1), (1, 0)])
 
@@ -370,9 +408,9 @@
     back = exchanged(jnp.broadcast_to(piece, wide.shape), FAR).reshape(rows, channels + LANES)
     small = back[:32, channels:].reshape(8, channels)
     back = jnp.concatenate([back[:, :channels], small], axis=0)
-    out = exchanged(jnp.broadcast_to(back, summed.shape), NEAR).astype(f32)
-    small = out[:, rows:rows + 3].reshape(cells, 3 * QUARTERS, channels)
-    return out[:, :rows].reshape(cells, channels, channels), small[:, :9], small[:, 9]
+    out = exchanged(jnp.broadcast_to(back, summed.shape), NEAR)
+    grad_point, grad_depth, grad_gain = widened(out, cells, channels)
+    return grad_point, jnp.transpose(grad_depth, (1, 0, 2)), grad_gain
 
 
 def solution(mesh):

time: 141 us -> 143 us (1.014)
  Pallas kernels: 14 us -> 20.7 us
  local copies, waits for them, and re-layouts: 4.27 us -> 0.3 us
    pallas_call x1, Pallas kernels: 14 us -> 17.9 us  [run_cells(): pl.pallas_call(cells_kernel, grid_spec=spec, out_shape=[out, out], compil...]
    pallas_call x0 -> x1, Pallas kernels: none -> 2.78 us  [widened(): pl.pallas_call(widen_kernel, in_specs=[pl.BlockSpec(memory_space=pltpu.VM...]
    slice x3 -> x0, local copies, waits for them, and re-layouts: 2.64 us -> none  [the longest x1 2.61 us: local(): out[:, :rows].reshape(cells, channels, channels)]
where the time goes in v5:
time: 143 us
  blocking collectives  107 us (75%)
  Pallas kernels  20.7 us (14%)
  starting transfers between devices  6.6 us (5%)
  waiting for transfers between devices  4.88 us (3%)
  other arithmetic  2.1 us (1%)
    all_to_all x4, blocking collectives, exchanged(): return lax.all_to_all(block, axes, 0, 0, tiled=True)  107 us
    pallas_call x1, Pallas kernels, run_cells(): pl.pallas_call(cells_kernel, grid_spec=spec, out_shape=[out, out], compil...  17.9 us
    ppermute x3, starting transfers between devices, swapped(): return lax.ppermute(block, 'section', [(0, 1), (1, 0)])  6.6 us
    ppermute x3, waiting for transfers between devices, swapped(): return lax.ppermute(block, 'section', [(0, 1), (1, 0)])  4.88 us
  transfers between devices with their start and end apart: 3, of which 2 were waited for; matrix products, arithmetic and copies ran while one was open for 1% of the time, Pallas kernels for 0%

profile of v5, /device:TPU:2, one launch (start us, length us, event | category | flops | bytes accessed | tf_op | source)
XLA Modules:
  0.0 143.3 jit_solution(6425005716067104855)
XLA Ops:
  0.6 1.9 %collective-permute-start.1 = (bf16[4,512,512]{2,1,0:T(8,128)(2,1)}, bf16[4,512,512]{2,1,0:T(8,128)(2,1)S(1)}, u32[]{:S(2)}, u32[]{:S(2)}) collective-permute-start(bf16[4,512,512]{2,1,0:T(8,128)(2,1)} %point_own.1), channel_id=1, source_target_pairs={{0,256},{256,0},{1,257},{257,1},{2,258},{258,2},{3,259},{259,3},{4... | collective-permute-start | bytes 6291464 | tf_op jit(solution)/shard_map/ppermute | solution.py:369
  3.2 0.1 pad.12.clone
  3.3 1.0 maximum_maximum_fusion.vec_own
  4.3 2.4 %collective-permute-start = (f32[11,4,512]{2,1,0:T(4,128)S(1)}, f32[11,4,512]{2,1,0:T(4,128)S(1)}, u32[]{:S(2)}, u32[]{:S(2)}) collective-permute-start(f32[11,4,512]{2,1,0:T(4,128)S(1)} %maximum_maximum_fusion.vec_own), channel_id=1, source_target_pairs={{0,256},{256,0},{1,257},{257,1},{2,258},{258,2},{3,259},{259,3},{4... | collective-permute-start | bytes 270344 | tf_op jit(solution)/shard_map/ppermute | solution.py:369
  6.7 0.9 collective-permute-done.vec_far
  7.6 0.0 collective-permute-done.1.point_far
  7.6 17.9 %cells.1 = (bf16[16,136,512]{2,1,0:T(8,128)(2,1)S(1)}, bf16[16,136,512]{2,1,0:T(8,128)(2,1)S(1)}) custom-call(s32[1]{0:T(128)} %bitcast.where_, bf16[4,2,8,8,512]{4,3,2,1,0:T(8,128)(2,1)} %images.1, bf16[4,2,8,8,512]{4,3,2,1,0:T(8,128)(2,1)} %cotangent.1, f32[11,4,512]{2,1,0:T(4,128)S(1)} %maximum_maximum_fusion.vec_own, ...), custom_call_target="tpu_custom_call" | custom-call | tf_op jit(solution)/shard_map/cells/pallas_call | solution.py:321
  25.5 2.3 %collective-permute-start.2 = (bf16[16,136,512]{2,1,0:T(8,128)(2,1)S(1)}, bf16[16,136,512]{2,1,0:T(8,128)(2,1)S(1)}, u32[]{:S(2)}, u32[]{:S(2)}) collective-permute-start(bf16[16,136,512]{2,1,0:T(8,128)(2,1)S(1)} %get-tuple-element.9), channel_id=1, source_target_pairs={{0,256},{256,0},{1,257},{257,1},{2,258},{258,2},{3,259},{259,3},{4... | collective-permute-start | bytes 6684680 | tf_op jit(solution)/shard_map/ppermute | solution.py:369
  27.8 4.0 %collective-permute-done.2 = bf16[16,136,512]{2,1,0:T(8,128)(2,1)S(1)} collective-permute-done((bf16[16,136,512]{2,1,0:T(8,128)(2,1)S(1)}, bf16[16,136,512]{2,1,0:T(8,128)(2,1)S(1)}, u32[]{:S(2)}, u32[]{:S(2)}) %collective-permute-start.2) | collective-permute-done | bytes 2228256 | tf_op jit(solution)/shard_map/ppermute | solution.py:369
  31.8 0.7 add_convert_fusion
  32.5 37.3 %all_to_all.20 = bf16[16,136,512]{2,1,0:T(8,128)(2,1)S(1)} all-to-all(bf16[16,136,512]{2,1,0:T(8,128)(2,1)S(1)} %add_convert_fusion), channel_id=1, replica_groups=mesh['section'=2,'zh'=4,'zl'=2,'yh'=4,'yl'=2,'x'=4] {'zl','yl','x'}, dimensions={0} | all-to-all | bytes 4456448 | tf_op jit(solution)/shard_map/all_to_all | solution.py:373
  69.8 0.3 reduce.1
  70.2 25.0 %all_to_all.21 = bf16[16,8,640]{2,1,0:T(8,128)(2,1)S(1)} all-to-all(bf16[16,8,640]{2,1,0:T(8,128)(2,1)S(1)} %pad_maximum_fusion), channel_id=1, replica_groups=mesh['section'=2,'zh'=4,'zl'=2,'yh'=4,'yl'=2,'x'=4] {'zh','yh'}, dimensions={0} | all-to-all | bytes 327680 | tf_op jit(solution)/shard_map/all_to_all | solution.py:373
  95.3 16.1 %all_to_all.22 = bf16[16,8,640]{2,1,0:T(8,128)(2,1)S(1)} all-to-all(bf16[16,8,640]{2,1,0:T(8,128)(2,1)S(1)} %broadcast_in_dim.24), channel_id=1, replica_groups=mesh['section'=2,'zh'=4,'zl'=2,'yh'=4,'yl'=2,'x'=4] {'zh','yh'}, dimensions={0} | all-to-all | bytes 327680 | tf_op jit(solution)/shard_map/all_to_all | solution.py:373
  111.5 0.1 broadcast_in_dim.25
  111.6 28.9 %all_to_all.23.totals = bf16[16,136,512]{2,1,0:T(8,128)(2,1)S(1)} all-to-all(bf16[16,136,512]{2,1,0:T(8,128)(2,1)S(1)} %broadcast_in_dim.25), channel_id=1, replica_groups=mesh['section'=2,'zh'=4,'zl'=2,'yh'=4,'yl'=2,'x'=4] {'zl','yl','x'}, dimensions={0} | all-to-all | bytes 4456448 | tf_op jit(solution)/shard_map/all_to_all | solution.py:373
  140.5 2.8 %widen.1 = (f32[4,512,512]{2,1,0:T(8,128)}, f32[9,4,512]{2,1,0:T(4,128)}, f32[4,512]{1,0:T(4,128)}) custom-call(bf16[16,136,512]{2,1,0:T(8,128)(2,1)S(1)} %all_to_all.23.totals), custom_call_target="tpu_custom_call" | custom-call | tf_op jit(solution)/shard_map/widen/pallas_call | solution.py:353
  (11 shorter events, 0.1 us)
Async XLA Ops:
  0.6 7.0 %collective-permute-start.1 = (bf16[4,512,512]{2,1,0:T(8,128)(2,1)}, bf16[4,512,512]{2,1,0:T(8,128)(2,1)S(1)}, u32[]{:S(2)}, u32[]{:S(2)}) collective-permute-start(bf16[4,512,512]{2,1,0:T(8,128)(2,1)} %point_own.1), channel_id=1, source_target_pairs={{0,256},{256,0},{1,257},{257,1},{2,258},{258,2},{3,259},{259,3},{4... | collective-permute-start | bytes 6291464 | tf_op jit(solution)/shard_map/ppermute | solution.py:369
  4.3 3.3 %collective-permute-start = (f32[11,4,512]{2,1,0:T(4,128)S(1)}, f32[11,4,512]{2,1,0:T(4,128)S(1)}, u32[]{:S(2)}, u32[]{:S(2)}) collective-permute-start(f32[11,4,512]{2,1,0:T(4,128)S(1)} %maximum_maximum_fusion.vec_own), channel_id=1, source_target_pairs={{0,256},{256,0},{1,257},{257,1},{2,258},{258,2},{3,259},{259,3},{4... | collective-permute-start | bytes 270344 | tf_op jit(solution)/shard_map/ppermute | solution.py:369
  25.5 6.2 %collective-permute-start.2 = (bf16[16,136,512]{2,1,0:T(8,128)(2,1)S(1)}, bf16[16,136,512]{2,1,0:T(8,128)(2,1)S(1)}, u32[]{:S(2)}, u32[]{:S(2)}) collective-permute-start(bf16[16,136,512]{2,1,0:T(8,128)(2,1)S(1)} %get-tuple-element.9), channel_id=1, source_target_pairs={{0,256},{256,0},{1,257},{257,1},{2,258},{258,2},{3,259},{259,3},{4... | collective-permute-start | bytes 6684680 | tf_op jit(solution)/shard_map/ppermute | solution.py:369

commit v6 on v5

--- a/solution.py
+++ b/solution.py
@@ -11,7 +11,7 @@
 f32, bf16 = jnp.float32, jnp.bfloat16
 LANES = 128
 QUARTERS = 4
-NEAR = ("zl", "yl", "x")
+NEAR = ("yl", "x", "zl")
 FAR = ("zh", "yh")
 
 

time: 143 us -> 140 us (0.979)
  the two profiles are of different devices: /device:TPU:2 before, /device:TPU:16 now
where the time goes in v6:
time: 140 us; the launch traced here: 137 us
  blocking collectives  107 us (76%)
  Pallas kernels  14.7 us (10%)
  starting transfers between devices  6.59 us (5%)
  waiting for transfers between devices  4.88 us (3%)
  other arithmetic  2.1 us (2%)
    all_to_all x4, blocking collectives, exchanged(): return lax.all_to_all(block, axes, 0, 0, tiled=True)  107 us
    pallas_call x1, Pallas kernels, run_cells(): pl.pallas_call(cells_kernel, grid_spec=spec, out_shape=[out, out], compil...  12 us
    ppermute x3, starting transfers between devices, swapped(): return lax.ppermute(block, 'section', [(0, 1), (1, 0)])  6.59 us
    ppermute x3, waiting for transfers between devices, swapped(): return lax.ppermute(block, 'section', [(0, 1), (1, 0)])  4.88 us
  transfers between devices with their start and end apart: 3, of which 2 were waited for; matrix products, arithmetic and copies ran while one was open for 1% of the time, Pallas kernels for 0%

profile of v6, /device:TPU:16, one launch (start us, length us, event | category | flops | bytes accessed | tf_op | source)
XLA Modules:
  0.0 137.3 jit_solution(7747810827228462002)
XLA Ops:
  0.6 1.9 %collective-permute-start.1 = (bf16[4,512,512]{2,1,0:T(8,128)(2,1)}, bf16[4,512,512]{2,1,0:T(8,128)(2,1)S(1)}, u32[]{:S(2)}, u32[]{:S(2)}) collective-permute-start(bf16[4,512,512]{2,1,0:T(8,128)(2,1)} %point_own.1), channel_id=1, source_target_pairs={{0,256},{256,0},{1,257},{257,1},{2,258},{258,2},{3,259},{259,3},{4... | collective-permute-start | bytes 6291464 | tf_op jit(solution)/shard_map/ppermute | solution.py:369
  3.2 0.1 pad.12.clone
  3.3 1.0 maximum_maximum_fusion.vec_own
  4.3 2.4 %collective-permute-start = (f32[11,4,512]{2,1,0:T(4,128)S(1)}, f32[11,4,512]{2,1,0:T(4,128)S(1)}, u32[]{:S(2)}, u32[]{:S(2)}) collective-permute-start(f32[11,4,512]{2,1,0:T(4,128)S(1)} %maximum_maximum_fusion.vec_own), channel_id=1, source_target_pairs={{0,256},{256,0},{1,257},{257,1},{2,258},{258,2},{3,259},{259,3},{4... | collective-permute-start | bytes 270344 | tf_op jit(solution)/shard_map/ppermute | solution.py:369
  6.7 0.9 collective-permute-done.vec_far
  7.6 0.0 collective-permute-done.1.point_far
  7.6 12.0 %cells.1 = (bf16[16,136,512]{2,1,0:T(8,128)(2,1)S(1)}, bf16[16,136,512]{2,1,0:T(8,128)(2,1)S(1)}) custom-call(s32[1]{0:T(128)} %bitcast.where_, bf16[4,2,8,8,512]{4,3,2,1,0:T(8,128)(2,1)} %images.1, bf16[4,2,8,8,512]{4,3,2,1,0:T(8,128)(2,1)} %cotangent.1, f32[11,4,512]{2,1,0:T(4,128)S(1)} %maximum_maximum_fusion.vec_own, ...), custom_call_target="tpu_custom_call" | custom-call | tf_op jit(solution)/shard_map/cells/pallas_call | solution.py:321
  19.6 2.3 %collective-permute-start.2 = (bf16[16,136,512]{2,1,0:T(8,128)(2,1)S(1)}, bf16[16,136,512]{2,1,0:T(8,128)(2,1)S(1)}, u32[]{:S(2)}, u32[]{:S(2)}) collective-permute-start(bf16[16,136,512]{2,1,0:T(8,128)(2,1)S(1)} %get-tuple-element.9), channel_id=1, source_target_pairs={{0,256},{256,0},{1,257},{257,1},{2,258},{258,2},{3,259},{259,3},{4... | collective-permute-start | bytes 6684680 | tf_op jit(solution)/shard_map/ppermute | solution.py:369
  21.8 4.0 %collective-permute-done.2 = bf16[16,136,512]{2,1,0:T(8,128)(2,1)S(1)} collective-permute-done((bf16[16,136,512]{2,1,0:T(8,128)(2,1)S(1)}, bf16[16,136,512]{2,1,0:T(8,128)(2,1)S(1)}, u32[]{:S(2)}, u32[]{:S(2)}) %collective-permute-start.2) | collective-permute-done | bytes 2228256 | tf_op jit(solution)/shard_map/ppermute | solution.py:369
  25.8 0.7 add_convert_fusion
  26.5 36.8 %all_to_all.20 = bf16[16,136,512]{2,1,0:T(8,128)(2,1)S(1)} all-to-all(bf16[16,136,512]{2,1,0:T(8,128)(2,1)S(1)} %add_convert_fusion), channel_id=1, replica_groups=mesh['section'=2,'zh'=4,'zl'=2,'yh'=4,'yl'=2,'x'=4] {'yl','x','zl'}, dimensions={0} | all-to-all | bytes 4456448 | tf_op jit(solution)/shard_map/all_to_all | solution.py:373
  63.3 0.3 reduce.1
  63.8 24.6 %all_to_all.21 = bf16[16,8,640]{2,1,0:T(8,128)(2,1)S(1)} all-to-all(bf16[16,8,640]{2,1,0:T(8,128)(2,1)S(1)} %pad_maximum_fusion), channel_id=1, replica_groups=mesh['section'=2,'zh'=4,'zl'=2,'yh'=4,'yl'=2,'x'=4] {'zh','yh'}, dimensions={0} | all-to-all | bytes 327680 | tf_op jit(solution)/shard_map/all_to_all | solution.py:373
  88.5 16.3 %all_to_all.22 = bf16[16,8,640]{2,1,0:T(8,128)(2,1)S(1)} all-to-all(bf16[16,8,640]{2,1,0:T(8,128)(2,1)S(1)} %broadcast_in_dim.24), channel_id=1, replica_groups=mesh['section'=2,'zh'=4,'zl'=2,'yh'=4,'yl'=2,'x'=4] {'zh','yh'}, dimensions={0} | all-to-all | bytes 327680 | tf_op jit(solution)/shard_map/all_to_all | solution.py:373
  104.8 0.1 broadcast_in_dim.25
  105.0 29.5 %all_to_all.23.totals = bf16[16,136,512]{2,1,0:T(8,128)(2,1)S(1)} all-to-all(bf16[16,136,512]{2,1,0:T(8,128)(2,1)S(1)} %broadcast_in_dim.25), channel_id=1, replica_groups=mesh['section'=2,'zh'=4,'zl'=2,'yh'=4,'yl'=2,'x'=4] {'yl','x','zl'}, dimensions={0} | all-to-all | bytes 4456448 | tf_op jit(solution)/shard_map/all_to_all | solution.py:373
  134.5 2.8 %widen.1 = (f32[4,512,512]{2,1,0:T(8,128)}, f32[9,4,512]{2,1,0:T(4,128)}, f32[4,512]{1,0:T(4,128)}) custom-call(bf16[16,136,512]{2,1,0:T(8,128)(2,1)S(1)} %all_to_all.23.totals), custom_call_target="tpu_custom_call" | custom-call | tf_op jit(solution)/shard_map/widen/pallas_call | solution.py:353
  (11 shorter events, 0.1 us)
Async XLA Ops:
  0.6 7.0 %collective-permute-start.1 = (bf16[4,512,512]{2,1,0:T(8,128)(2,1)}, bf16[4,512,512]{2,1,0:T(8,128)(2,1)S(1)}, u32[]{:S(2)}, u32[]{:S(2)}) collective-permute-start(bf16[4,512,512]{2,1,0:T(8,128)(2,1)} %point_own.1), channel_id=1, source_target_pairs={{0,256},{256,0},{1,257},{257,1},{2,258},{258,2},{3,259},{259,3},{4... | collective-permute-start | bytes 6291464 | tf_op jit(solution)/shard_map/ppermute | solution.py:369
  4.3 3.3 %collective-permute-start = (f32[11,4,512]{2,1,0:T(4,128)S(1)}, f32[11,4,512]{2,1,0:T(4,128)S(1)}, u32[]{:S(2)}, u32[]{:S(2)}) collective-permute-start(f32[11,4,512]{2,1,0:T(4,128)S(1)} %maximum_maximum_fusion.vec_own), channel_id=1, source_target_pairs={{0,256},{256,0},{1,257},{257,1},{2,258},{258,2},{3,259},{259,3},{4... | collective-permute-start | bytes 270344 | tf_op jit(solution)/shard_map/ppermute | solution.py:369
  19.6 6.2 %collective-permute-start.2 = (bf16[16,136,512]{2,1,0:T(8,128)(2,1)S(1)}, bf16[16,136,512]{2,1,0:T(8,128)(2,1)S(1)}, u32[]{:S(2)}, u32[]{:S(2)}) collective-permute-start(bf16[16,136,512]{2,1,0:T(8,128)(2,1)S(1)} %get-tuple-element.9), channel_id=1, source_target_pairs={{0,256},{256,0},{1,257},{257,1},{2,258},{258,2},{3,259},{259,3},{4... | collective-permute-start | bytes 6684680 | tf_op jit(solution)/shard_map/ppermute | solution.py:369
